TPU v7x, 32 devices: a whole 2x2x4 slice. The times are simulated.
32 devices in a mesh: dp: 8 (over y, x, core), ctx: 4 (over z).
Axes of the slice: x: 2, y: 2, z: 4, core: 2. Of those that a mesh axis runs over, the one named last changes fastest.
Arguments:
- tokens: bfloat16 [2, 8, 1024, 1024], P(None, 'dp', 'ctx'), may hold values from -6 to 6
- segments: int32 [2, 8, 1024], P(None, 'dp', 'ctx'), may hold values from 0 to 18, as said below
- cotangent: bfloat16 [2, 8, 1024, 1024], P(None, 'dp', 'ctx'), may hold values from -6 to 6
- attn_gain: bfloat16 [1024], P(('dp', 'ctx')), may hold values from 0.5 to 1.5
- w_qkv: bfloat16 [1024, 3072], P(('dp', 'ctx')), may hold values from -0.1875 to 0.1875
- w_attn_out: bfloat16 [1024, 1024], P(('dp', 'ctx')), may hold values from -3 to 3
- mlp_gain: bfloat16 [1024], P(('dp', 'ctx')), may hold values from 0.5 to 1.5
- w_in: bfloat16 [1024, 5248], P(('dp', 'ctx')), may hold values from -0.1875 to 0.1875
- w_mlp_out: bfloat16 [1024, 2624], P(('dp', 'ctx')), may hold values from -0.25 to 0.25
Outputs:
- layer_out: bfloat16 [2, 8, 1024, 1024], P(None, 'dp', 'ctx')
- input_grad: bfloat16 [2, 8, 1024, 1024], P(None, 'dp', 'ctx')
- attn_gain_grad: float32 [1024], P(('dp', 'ctx'))
- qkv_grad: float32 [1024, 3072], P(('dp', 'ctx'))
- attn_out_grad: float32 [1024, 1024], P(('dp', 'ctx'))
- mlp_gain_grad: float32 [1024], P(('dp', 'ctx'))
- in_grad: float32 [1024, 5248], P(('dp', 'ctx'))
- mlp_out_grad: float32 [1024, 2624], P(('dp', 'ctx'))
Inputs may be any that keep to these rules, and one draw needn't show every extreme that they name: `segments`: in each sequence, ids 1, 2, 3 and so on number its documents in order, each of 60 to 800 tokens except the last, which may be cut shorter; a tail of segment 0 of at least one token ends every sequence.
All inputs are finite; a program needn't handle non-finite values.
Results may differ from a plain program's by a relative error of at most 0.017.
Values may be sent and summed in bfloat16 or wider, within the bound.
No kernel may reach another device: no remote copies, remote signals or barrier semaphores. Data moves between devices by JAX's collectives and lax.ppermute only.
A program may use at most 256 MiB of HBM per device.

v0:
```python
import functools
import math

import jax
import jax.numpy as jnp
from jax import lax
from jax.experimental import pallas as pl
from jax.experimental.pallas import tpu as pltpu
from jax.sharding import PartitionSpec as P

HEADS = 16
HEAD = 64
LANE = 128

epsilon = 1e-05
rope_base = 160000.0
NEG = -1e30
LOG2E = math.log2(math.e)

COST = pl.CostEstimate(flops=1, transcendentals=0, bytes_accessed=1)
F32 = jnp.float32
BF16 = jnp.bfloat16
ANY = pl.BlockSpec(memory_space=pl.ANY)
SMEM = pl.BlockSpec(memory_space=pltpu.SMEM)


def params(*, mib=56):
    return pltpu.CompilerParams(vmem_limit_bytes=mib << 20)


def sds(shape, dtype):
    return jax.ShapeDtypeStruct(shape, dtype)


def nt(a, b):
    return lax.dot_general(a, b, (((1,), (1,)), ((), ())), preferred_element_type=F32)


def nn(a, b):
    return lax.dot_general(a, b, (((1,), (0,)), ((), ())), preferred_element_type=F32)


def lanes(perm, m):
    return pl.ds(pl.multiple_of(perm[m] * LANE, LANE), LANE)


def tn(a, b):
    return lax.dot_general(a, b, (((0,), (0,)), ((), ())), preferred_element_type=F32)


def chunks(count, size=1024):
    return [(c, min(size, count - c)) for c in range(0, count, size)]


class Copies:
    def __init__(self, sems):
        self.sems, self.used = sems, 0

    def start(self, source, target):
        copy = pltpu.make_async_copy(source, target, self.sems.at[self.used])
        self.used += 1
        copy.start()
        return [copy]

    def weight(self, pieces, col, count, target, to=None):
        out = []
        to = col if to is None else to
        for m, piece in enumerate(pieces):
            rows = piece.shape[0]
            out += self.start(piece.at[:, col : col + count], target.at[m * rows : (m + 1) * rows, to : to + count])
        return out


def joined(move, parts, cut, start, count, target, to):
    low = max(0, min(count, cut - start))
    out = move.weight(parts[0], start, low, target, to) if low else []
    if low < count:
        out += move.weight(parts[1], start + low - cut, count - low, target, to + low)
    return out


def wait(copies):
    for c in copies:
        c.wait()


def row_tiles(rows, tile, body):
    def step(i, carry):
        body(pl.ds(pl.multiple_of(i * tile, tile), tile))
        return carry

    lax.fori_loop(0, rows // tile, step, 0)


def call(body, perm, small, big, outs, scratch, copies, name):
    return pl.pallas_call(
        body,
        out_shape=tuple(outs),
        in_specs=[SMEM] + [pl.BlockSpec(memory_space=pltpu.VMEM)] * len(small) + [ANY] * len(big),
        out_specs=(ANY,) * len(outs),
        scratch_shapes=[*scratch, pltpu.SemaphoreType.DMA((copies,))],
        compiler_params=params(),
        cost_estimate=COST,
        name=name,
    )(perm, *small, *big)


def norm_rows(v):
    centered = v - jnp.mean(v, axis=-1, keepdims=True)
    inv = lax.rsqrt(jnp.mean(centered * centered, axis=-1, keepdims=True) + epsilon)
    return centered * inv, inv


def turn(u, cos, sin):
    first = lax.broadcasted_iota(jnp.int32, (1, LANE), 1) % HEAD < HEAD // 2
    out = []
    for h in range(u.shape[1] // LANE):
        b = u[:, h * LANE : (h + 1) * LANE]
        t = jnp.where(first, pltpu.roll(b, LANE - HEAD // 2, 1), pltpu.roll(b, HEAD // 2, 1))
        out.append(b * cos + t * sin)
    return jnp.concatenate(out, axis=1)


def qkv_body(n, perm, cos_ref, sin_ref, x_hbm, *rest):
    p0, p1 = rest[:n], rest[n : 2 * n]
    a_hbm, q_hbm, kv_hbm, gains_hbm, x, w, g, gains, a, ap, out, sems = rest[2 * n :]
    move = Copies(sems)
    rows, width = x.shape
    half = width // 2
    got_x = move.start(x_hbm, x)
    got_gains = move.weight(p0, 3 * half, LANE, g, 0)
    got = [move.weight(p, c * half, half, w, (3 * i + c) * half) for i, p in enumerate((p0, p1)) for c in range(3)]
    wait(got_gains)
    for m in range(width // LANE):
        gains[:, lanes(perm, m)] = g[m * LANE : (m + 1) * LANE, :].astype(F32).T[0:8, :]
    done = move.start(gains, gains_hbm)
    wait(got_x)

    def normalize(r):
        normed, _ = norm_rows(x[r, :].astype(F32))
        a[r, :] = (normed * gains[0:1, :]).astype(BF16)

    row_tiles(rows, LANE, normalize)
    done += move.start(a, a_hbm)
    for m in range(width // LANE):
        ap[:, m * LANE : (m + 1) * LANE] = a[:, lanes(perm, m)]
    for c in range(6):
        cols = slice(c * half, (c + 1) * half)
        kind, part = c % 3, c // 3
        wait(got[c])

        def project(r, cols=cols, kind=kind):
            u = nn(ap[r, :], w[:, cols])
            if kind < 2:
                u = turn(u, cos_ref[r, :], sin_ref[r, :])
            out[r, cols] = u.astype(BF16)

        row_tiles(rows, min(512, rows), project)
        if kind == 0:
            done += move.start(out.at[:, cols], q_hbm.at[:, part * half : (part + 1) * half])
        else:
            to = (kind - 1) * width + part * half
            done += move.start(out.at[:, cols], kv_hbm.at[:, to : to + half])
    wait(done)


def qkv_call(perm, x, cos, sin, p0, p1):
    rows, width = x.shape
    return call(
        functools.partial(qkv_body, len(p0)),
        perm,
        [cos, sin],
        [x, *p0, *p1],
        [sds((rows, width), BF16), sds((rows, width), BF16), sds((rows, 2 * width), BF16), sds((8, width), F32)],
        [
            pltpu.VMEM((rows, width), BF16),
            pltpu.VMEM((width, 3 * width), BF16),
            pltpu.VMEM((width, LANE), BF16),
            pltpu.VMEM((8, width), F32),
            pltpu.VMEM((rows, width), BF16),
            pltpu.VMEM((rows, width), BF16),
            pltpu.VMEM((rows, 3 * width), BF16),
        ],
        9 + 7 * len(p0),
        "qkv",
    )


def attend_body(perm, segk_ref, segq_ref, q_ref, k0_ref, k1_ref, v0_ref, v1_ref, o_ref, p_ref, bias, vt):
    j = pl.program_id(0)
    rows = q_ref.shape[0]
    tile = min(512, rows)

    @pl.when(j == 0)
    def _():
        bias[...] = jnp.where(segk_ref[:, :1] == segq_ref[...], 0.0, NEG)

    for i in range(rows // LANE):
        r = slice(i * LANE, (i + 1) * LANE)
        vt[:, r] = v0_ref[r, :].astype(F32).T.astype(BF16)
        vt[:, rows + i * LANE : rows + (i + 1) * LANE] = v1_ref[r, :].astype(F32).T.astype(BF16)
    head_of = lax.broadcasted_iota(jnp.int32, (1, LANE), 1) // HEAD
    scale = LOG2E / math.sqrt(HEAD)
    for t in range(rows // tile):
        cols = slice(t * tile, (t + 1) * tile)
        q = q_ref[cols, :]
        parts = []
        for h in range(LANE // HEAD):
            qm = jnp.where(head_of == h, q, jnp.zeros_like(q))
            s = jnp.concatenate([nt(k0_ref[...], qm), nt(k1_ref[...], qm)], axis=0) * scale + bias[:, cols]
            top = jnp.max(s, axis=0, keepdims=True)
            e = jnp.exp2(s - top)
            total = jnp.sum(e, axis=0, keepdims=True)
            p = (e * (1.0 / total)).astype(BF16)
            p_ref[0, h, :, cols] = p
            parts.append(nn(vt[...], p)[h * HEAD : (h + 1) * HEAD, :])
        o_ref[cols, :] = jnp.concatenate(parts, axis=0).T.astype(BF16)


def attend_call(perm, segk, segq, q, kv0, kv1, first, count):
    rows, width = q.shape
    pairs = width // LANE
    full = lambda j: (0, 0)
    at = lambda j: (0, first + j)
    vat = lambda j: (0, pairs + first + j)
    block = (rows, LANE)
    heads = LANE // HEAD
    return pl.pallas_call(
        attend_body,
        grid=(count,),
        out_shape=(sds((rows, count * LANE), BF16), sds((count, heads, 2 * rows, rows), BF16)),
        in_specs=[
            SMEM,
            pl.BlockSpec((2 * rows, LANE), full),
            pl.BlockSpec((1, rows), full),
            pl.BlockSpec(block, at),
            pl.BlockSpec(block, at),
            pl.BlockSpec(block, at),
            pl.BlockSpec(block, vat),
            pl.BlockSpec(block, vat),
        ],
        out_specs=(
            pl.BlockSpec(block, lambda j: (0, j)),
            pl.BlockSpec((1, heads, 2 * rows, rows), lambda j: (j, 0, 0, 0)),
        ),
        scratch_shapes=[pltpu.VMEM((2 * rows, rows), F32), pltpu.VMEM((LANE, 2 * rows), BF16)],
        compiler_params=params(),
        cost_estimate=COST,
        name="attend",
    )(perm, segk, segq, q, kv0, kv1, kv0, kv1)


def middle_body(n, perm, gains_ref, keep_ref, x_hbm, oa_hbm, ob_hbm, *rest):
    pieces = rest[:n]
    h1_hbm, b_hbm, o_hbm, x, o, op, w, h1, b, sems = rest[n:]
    move = Copies(sems)
    rows, width = x.shape
    half = width // 2
    got = move.start(oa_hbm, o.at[:, :half]) + move.start(ob_hbm, o.at[:, half:])
    got += move.weight(pieces, 0, width, w) + move.start(x_hbm, x)
    wait(got[:2])
    done = move.start(o, o_hbm)
    for m in range(width // LANE):
        op[:, m * LANE : (m + 1) * LANE] = o[:, lanes(perm, m)]
    wait(got[2:])
    for t in range(2):
        base = t * (rows // 2)

        def tile(i, carry, base=base):
            r = pl.ds(pl.multiple_of(base + i * 256, 256), 256)
            v = x[r, :].astype(F32) + keep_ref[r, :1] * nn(op[r, :], w[...])
            h1[r, :] = v
            normed, _ = norm_rows(v)
            b[r, :] = (normed * gains_ref[1:2, :]).astype(BF16)
            return carry

        lax.fori_loop(0, rows // 2 // 256, tile, 0)
        part = slice(base, base + rows // 2)
        done += move.start(b.at[part, :], b_hbm.at[part, :]) + move.start(h1.at[part, :], h1_hbm.at[part, :])
    wait(done)


def middle_call(perm, gains, x, keep, oa, ob, pieces):
    rows, width = x.shape
    return call(
        functools.partial(middle_body, len(pieces)),
        perm,
        [gains, keep],
        [x, oa, ob, *pieces],
        [sds((rows, width), F32), sds((rows, width), BF16), sds((rows, width), BF16)],
        [
            pltpu.VMEM((rows, width), BF16),
            pltpu.VMEM((rows, width), BF16),
            pltpu.VMEM((rows, width), BF16),
            pltpu.VMEM((width, width), BF16),
            pltpu.VMEM((rows, width), F32),
            pltpu.VMEM((rows, width), BF16),
        ],
        8 + len(pieces),
        "middle",
    )


def gate_body(n, cut, base, perm, b_hbm, *rest):
    pa, pb = rest[:n], rest[n : 2 * n]
    m_hbm, f1_hbm, f2_hbm, b, bp, wg, wu, mv, f1, f2, sems = rest[2 * n :]
    move = Copies(sems)
    rows, width = b.shape
    parts = chunks(mv.shape[1])
    got_b = move.start(b_hbm, b)
    hidden = mv.shape[1]
    got = [
        joined(move, (pa, pb), cut, base + c, k, wg, c) + joined(move, (pa, pb), cut, base + hidden + c, k, wu, c)
        for c, k in parts
    ]
    wait(got_b)
    for m in range(width // LANE):
        bp[:, m * LANE : (m + 1) * LANE] = b[:, lanes(perm, m)]
    done = []
    for (c, k), g in zip(parts, got):
        cols = slice(c, c + k)
        wait(g)

        def tile(r, cols=cols):
            gate = nn(bp[r, :], wg[:, cols])
            up = nn(bp[r, :], wu[:, cols])
            cdf = 0.5 * (1.0 + lax.erf(gate * (1.0 / math.sqrt(2.0))))
            density = jnp.exp(-0.5 * gate * gate) * (1.0 / math.sqrt(2.0 * math.pi))
            act = gate * cdf
            mv[r, cols] = (act * up).astype(BF16)
            f1[r, cols] = (up * (cdf + gate * density)).astype(BF16)
            f2[r, cols] = act.astype(BF16)

        row_tiles(rows, min(512, rows), tile)
        for v, to in ((mv, m_hbm), (f1, f1_hbm), (f2, f2_hbm)):
            done += move.start(v.at[:, cols], to.at[:, cols])
    wait(done)


def gate_call(perm, b, pa, pb, hidden, base, cut):
    rows, width = b.shape
    return call(
        functools.partial(gate_body, len(pa), cut, base),
        perm,
        [],
        [b, *pa, *pb],
        [sds((rows, hidden), BF16)] * 3,
        [pltpu.VMEM((rows, width), BF16)] * 2 + [pltpu.VMEM((width, hidden), BF16)] * 2 + [pltpu.VMEM((rows, hidden), BF16)] * 3,
        1 + len(pa) + len(chunks(hidden)) * (2 * len(pa) + 3),
        "gate",
    )


def dgate_body(n, perm, keep_ref, cot_hbm, f1_hbm, f2_hbm, h1_hbm, m_hbm, *rest):
    pd = rest[:n]
    dg_hbm, du_hbm, out_hbm, cot, ep, wd, f1, f2, h1, mv, acc, out, sems = rest[n:]
    move = Copies(sems)
    rows, width = cot.shape
    parts = chunks(f1.shape[1])
    got_cot = move.start(cot_hbm, cot)
    got, got_m = [], []
    for c, k in parts:
        cols = slice(c, c + k)
        got.append(
            move.weight(pd, c, k, wd)
            + move.start(f1_hbm.at[:, cols], f1.at[:, cols])
            + move.start(f2_hbm.at[:, cols], f2.at[:, cols])
        )
    for c, k in parts:
        got_m.append(move.start(m_hbm.at[:, c : c + k], mv.at[:, c : c + k]))
    got_h1 = move.start(h1_hbm, h1)
    wait(got_cot)
    for m in range(width // LANE):
        ep[:, m * LANE : (m + 1) * LANE] = (keep_ref[...] * cot[:, lanes(perm, m)].astype(F32)).astype(BF16)
    done = []
    for (c, k), g in zip(parts, got):
        cols = slice(c, c + k)
        wait(g)

        def tile(r, cols=cols):
            dm = nn(ep[r, :], wd[:, cols])
            f1[r, cols] = (dm * f1[r, cols].astype(F32)).astype(BF16)
            f2[r, cols] = (dm * f2[r, cols].astype(F32)).astype(BF16)

        row_tiles(rows, min(512, rows), tile)
        done += move.start(f1.at[:, cols], dg_hbm.at[:, cols]) + move.start(f2.at[:, cols], du_hbm.at[:, cols])
    for i, ((c, k), g) in enumerate(zip(parts, got_m)):
        cols = slice(c, c + k)
        wait(g)

        def add(r, cols=cols, i=i):
            v = nt(mv[r, cols], wd[:, cols])
            acc[r, :] = v if i == 0 else acc[r, :] + v

        row_tiles(rows, min(512, rows), add)
    wait(got_h1)
    for m in range(width // LANE):
        at = lanes(perm, m)
        out[:, at] = (h1[:, at] + keep_ref[...] * acc[:, m * LANE : (m + 1) * LANE]).astype(BF16)
    done += move.start(out, out_hbm)
    wait(done)


def dgate_call(perm, cot, keep, f1, f2, h1, mixed, pd):
    rows, width = cot.shape
    hidden = f1.shape[1]
    return call(
        functools.partial(dgate_body, len(pd)),
        perm,
        [keep],
        [cot, f1, f2, h1, mixed, *pd],
        [sds((rows, hidden), BF16)] * 2 + [sds((rows, width), BF16)],
        [pltpu.VMEM((rows, width), BF16)] * 2
        + [pltpu.VMEM((width, hidden), BF16)]
        + [pltpu.VMEM((rows, hidden), BF16)] * 2
        + [
            pltpu.VMEM((rows, width), F32),
            pltpu.VMEM((rows, hidden), BF16),
            pltpu.VMEM((rows, width), F32),
            pltpu.VMEM((rows, width), BF16),
        ],
        3 + len(chunks(hidden)) * (len(pd) + 5),
        "dgate",
    )


def norm_back(e, gain, normed, inv):
    scaled = e * gain
    return inv * (
        scaled
        - jnp.mean(scaled, axis=-1, keepdims=True)
        - normed * jnp.mean(scaled * normed, axis=-1, keepdims=True)
    )


def dmiddle_body(n, cut, base, perm, gains_ref, keep_ref, cot_hbm, h1_hbm, dg_hbm, du_hbm, *rest):
    pa, pb = rest[:n], rest[n : 2 * n]
    dh1_hbm, e_hbm, do_hbm, gg_hbm, cot, h1, dg, du, wg, wu, wo, acc, db, e, do, gg, sems = rest[2 * n :]
    move = Copies(sems)
    rows, width = h1.shape
    parts = chunks(dg.shape[1])
    got = []
    for c, k in parts:
        cols = slice(c, c + k)
        got.append(move.start(dg_hbm.at[:, cols], dg.at[:, cols]) + joined(move, (pa, pb), cut, base + c, k, wg, c))
        at = base + dg.shape[1] + c
        got.append(move.start(du_hbm.at[:, cols], du.at[:, cols]) + joined(move, (pa, pb), cut, at, k, wu, c))
    got_rest = move.start(h1_hbm, h1) + move.start(cot_hbm, cot) + move.weight(pa, 0, width, wo)
    for i, g in enumerate(got):
        c, k = parts[i // 2]
        cols = slice(c, c + k)
        left, right = ((dg, wg), (du, wu))[i % 2]
        wait(g)

        def tile(r, cols=cols, left=left, right=right, i=i):
            v = nt(left[r, cols], right[:, cols])
            acc[r, :] = v if i == 0 else acc[r, :] + v

        row_tiles(rows, min(512, rows), tile)
    for m in range(width // LANE):
        db[:, lanes(perm, m)] = acc[:, m * LANE : (m + 1) * LANE]
    gg[...] = jnp.zeros_like(gg)
    wait(got_rest)
    done = []
    for t in range(2):
        at = t * (rows // 2)

        def back(i, carry, at=at):
            r = pl.ds(pl.multiple_of(at + i * LANE, LANE), LANE)
            normed, inv = norm_rows(h1[r, :])
            v = db[r, :]
            gg[...] += jnp.sum(v * normed, axis=0, keepdims=True)
            dh1 = cot[r, :].astype(F32) + norm_back(v, gains_ref[1:2, :], normed, inv)
            db[r, :] = dh1
            e[r, :] = (keep_ref[r, :1] * dh1).astype(BF16)
            return carry

        lax.fori_loop(0, rows // 2 // LANE, back, 0)
        part = slice(at, at + rows // 2)
        done += move.start(db.at[part, :], dh1_hbm.at[part, :]) + move.start(e.at[part, :], e_hbm.at[part, :])
        d = nt(e[part, :], wo[...])
        for m in range(width // LANE):
            do[part, lanes(perm, m)] = d[:, m * LANE : (m + 1) * LANE].astype(BF16)
        done += move.start(do.at[part, :], do_hbm.at[part, :])
    done += move.start(gg, gg_hbm)
    wait(done)


def dmiddle_call(perm, gains, cot, keep, h1, dg, du, pa, pb, base, cut):
    rows, width = h1.shape
    hidden = dg.shape[1]
    return call(
        functools.partial(dmiddle_body, len(pa), cut, base),
        perm,
        [gains, keep],
        [cot, h1, dg, du, *pa, *pb],
        [sds((rows, width), F32), sds((rows, width), BF16), sds((rows, width), BF16), sds((1, width), F32)],
        [
            pltpu.VMEM((rows, width), BF16),
            pltpu.VMEM((rows, width), F32),
            pltpu.VMEM((rows, hidden), BF16),
            pltpu.VMEM((rows, hidden), BF16),
            pltpu.VMEM((width, hidden), BF16),
            pltpu.VMEM((width, hidden), BF16),
            pltpu.VMEM((width, width), BF16),
            pltpu.VMEM((rows, width), F32),
            pltpu.VMEM((rows, width), F32),
            pltpu.VMEM((rows, width), BF16),
            pltpu.VMEM((rows, width), BF16),
            pltpu.VMEM((1, width), F32),
        ],
        9 + 2 * len(pa) + len(chunks(hidden)) * 2 * (len(pa) + 1),
        "dmiddle",
    )


def dattend_body(
    perm, q_ref, k0_ref, k1_ref, v0_ref, v1_ref, do_ref, p_ref, dq_ref, dk0_ref, dv0_ref, dk1_ref, dv1_ref, kt, dk, dv
):
    rows = q_ref.shape[0]
    tile = min(512, rows)
    for i in range(rows // LANE):
        r = slice(i * LANE, (i + 1) * LANE)
        kt[:, r] = k0_ref[r, :].astype(F32).T.astype(BF16)
        kt[:, rows + i * LANE : rows + (i + 1) * LANE] = k1_ref[r, :].astype(F32).T.astype(BF16)
    head_of = lax.broadcasted_iota(jnp.int32, (1, LANE), 1) // HEAD
    back = 1.0 / math.sqrt(HEAD)
    for t in range(rows // tile):
        cols = slice(t * tile, (t + 1) * tile)
        q = q_ref[cols, :]
        do = do_ref[cols, :]
        parts = []
        for h in range(LANE // HEAD):
            qm = jnp.where(head_of == h, q, jnp.zeros_like(q))
            dom = jnp.where(head_of == h, do, jnp.zeros_like(do))
            p = p_ref[0, h, :, cols]
            pf = p.astype(F32)
            dp = jnp.concatenate([nt(v0_ref[...], dom), nt(v1_ref[...], dom)], axis=0)
            inner = jnp.sum(pf * dp, axis=0, keepdims=True)
            ds = (pf * (dp - inner)).astype(BF16)
            dv_new = nn(p, dom)
            dk_new = nn(ds, qm)
            if t == 0 and h == 0:
                dv[...] = dv_new
                dk[...] = dk_new
            else:
                dv[...] += dv_new
                dk[...] += dk_new
            parts.append(nn(kt[...], ds)[h * HEAD : (h + 1) * HEAD, :])
        dq_ref[cols, :] = (jnp.concatenate(parts, axis=0).T * back).astype(BF16)
    dk0_ref[...] = dk[:rows, :]
    dv0_ref[...] = dv[:rows, :]
    dk1_ref[...] = dk[rows:, :].astype(BF16)
    dv1_ref[...] = dv[rows:, :].astype(BF16)


def dattend_call(perm, q, kv0, kv1, do, p, first):
    rows, width = q.shape
    pairs = width // LANE
    count = p.shape[0]
    at = lambda j: (0, first + j)
    vat = lambda j: (0, pairs + first + j)
    block = (rows, LANE)
    return pl.pallas_call(
        dattend_body,
        grid=(count,),
        out_shape=(
            sds((rows, count * LANE), BF16),
            sds((rows, count * LANE), F32),
            sds((rows, count * LANE), F32),
            sds((rows, count * LANE), BF16),
            sds((rows, count * LANE), BF16),
        ),
        in_specs=[
            SMEM,
            pl.BlockSpec(block, at),
            pl.BlockSpec(block, at),
            pl.BlockSpec(block, at),
            pl.BlockSpec(block, vat),
            pl.BlockSpec(block, vat),
            pl.BlockSpec(block, at),
            pl.BlockSpec((1, *p.shape[1:]), lambda j: (j, 0, 0, 0)),
        ],
        out_specs=(pl.BlockSpec(block, lambda j: (0, j)),) * 5,
        scratch_shapes=[
            pltpu.VMEM((LANE, 2 * rows), BF16),
            pltpu.VMEM((2 * rows, LANE), F32),
            pltpu.VMEM((2 * rows, LANE), F32),
        ],
        compiler_params=params(),
        cost_estimate=COST,
        name="dattend",
    )(perm, q, kv0, kv1, kv0, kv1, do, p)


def dqkv_body(perm, cos_ref, sin_ref, dq_ref, dk0_ref, dv0_ref, dk1_ref, dv1_ref, out_ref):
    width = dq_ref.shape[1]
    cos = cos_ref[...]
    sin = -sin_ref[...]
    out_ref[:, :width] = turn(dq_ref[...].astype(F32), cos, sin).astype(BF16)
    key = ((dk0_ref[...] + dk1_ref[...].astype(F32)) * (1.0 / math.sqrt(HEAD))).astype(BF16)
    out_ref[:, width : 2 * width] = turn(key.astype(F32), cos, sin).astype(BF16)
    out_ref[:, 2 * width :] = (dv0_ref[...] + dv1_ref[...].astype(F32)).astype(BF16)


def dqkv_call(perm, cos, sin, dq, dk0, dv0, dk1, dv1):
    rows, width = dq.shape
    tile = 256
    row = lambda i: (i, 0)
    block = pl.BlockSpec((tile, width), row)
    return pl.pallas_call(
        dqkv_body,
        grid=(rows // tile,),
        out_shape=sds((rows, 3 * width), BF16),
        in_specs=[SMEM] + [pl.BlockSpec((tile, LANE), row)] * 2 + [block] * 5,
        out_specs=pl.BlockSpec((tile, 3 * width), row),
        compiler_params=params(),
        cost_estimate=COST,
        name="dqkv",
    )(perm, cos, sin, dq, dk0, dv0, dk1, dv1)


def dinput_body(n, perm, gains_ref, x_hbm, dh1_hbm, da_hbm, db_hbm, *rest):
    p0, p1 = rest[:n], rest[n : 2 * n]
    out_hbm, gg_hbm, x, dh1, d, w, acc, e, out, gg, sems = rest[2 * n :]
    move = Copies(sems)
    rows, width = x.shape
    part = 3 * width // 2
    got = []
    for i, (source, pieces) in enumerate(((da_hbm, p0), (db_hbm, p1))):
        for c, k in chunks(part, part // 2):
            to = slice(i * part + c, i * part + c + k)
            got.append((to, move.start(source.at[:, c : c + k], d.at[:, to]) + move.weight(pieces, c, k, w, i * part + c)))
    got_rest = move.start(x_hbm, x) + move.start(dh1_hbm, dh1)
    for i, (cols, g) in enumerate(got):
        wait(g)

        def tile(r, cols=cols, i=i):
            v = nt(d[r, cols], w[:, cols])
            acc[r, :] = v if i == 0 else acc[r, :] + v

        row_tiles(rows, min(512, rows), tile)
    for m in range(width // LANE):
        e[:, lanes(perm, m)] = acc[:, m * LANE : (m + 1) * LANE]
    gg[...] = jnp.zeros_like(gg)
    wait(got_rest)
    done = []
    for t in range(2):
        at = t * (rows // 2)

        def back(i, carry, at=at):
            r = pl.ds(pl.multiple_of(at + i * LANE, LANE), LANE)
            normed, inv = norm_rows(x[r, :].astype(F32))
            v = e[r, :]
            gg[...] += jnp.sum(v * normed, axis=0, keepdims=True)
            out[r, :] = (dh1[r, :] + norm_back(v, gains_ref[0:1, :], normed, inv)).astype(BF16)
            return carry

        lax.fori_loop(0, rows // 2 // LANE, back, 0)
        here = slice(at, at + rows // 2)
        done += move.start(out.at[here, :], out_hbm.at[here, :])
    done += move.start(gg, gg_hbm)
    wait(done)


def dinput_call(perm, gains, x, dh1, da, db, p0, p1):
    rows, width = x.shape
    return call(
        functools.partial(dinput_body, len(p0)),
        perm,
        [gains],
        [x, dh1, da, db, *p0, *p1],
        [sds((rows, width), BF16), sds((1, width), F32)],
        [
            pltpu.VMEM((rows, width), BF16),
            pltpu.VMEM((rows, width), F32),
            pltpu.VMEM((rows, 3 * width), BF16),
            pltpu.VMEM((width, 3 * width), BF16),
            pltpu.VMEM((rows, width), F32),
            pltpu.VMEM((rows, width), F32),
            pltpu.VMEM((rows, width), BF16),
            pltpu.VMEM((1, width), F32),
        ],
        9 + 4 * len(p0),
        "dinput",
    )


def grad_body(masked, forms, col, perm, *refs):
    count = 2 if forms[0] != "f" else 1
    keeps = refs[: count if masked else 0]
    refs = refs[len(keeps) :]
    lefts, rights = refs[:count], refs[count : count * (1 + len(forms))]
    outs = refs[count * (1 + len(forms)) : -4]
    left, right, out, sems = refs[-4:]
    per = len(outs) // len(forms)
    move = Copies(sems)
    height, width = left.shape[2], right.shape[2]
    parts = chunks(width)
    got_left, got = [[] for _ in range(count)], [[[] for _ in parts] for _ in forms]
    for f in range(len(forms)):
        for p, (c, k) in enumerate(parts):
            for s in range(count):
                if f == 0 and p == 0:
                    for i in range(height // LANE):
                        block = left.at[s, :, i * LANE : (i + 1) * LANE]
                        got_left[s] += move.start(lefts[s].at[:, lanes(perm, i)], block)
                source = rights[f * count + s].at[:, col + c : col + c + k]
                got[f][p] += move.start(source, right.at[f * count + s, :, c : c + k])
    for s in range(count):
        wait(got_left[s])
        if masked:
            left[s] = (left[s].astype(F32) * keeps[s][:, :1]).astype(BF16)
    done = []
    for f, form in enumerate(forms):
        for (c, k), g in zip(parts, got[f]):
            cols = slice(c, c + k)
            wait(g)
            for t in range(height // 256):
                rows = slice(t * 256, (t + 1) * 256)
                v = tn(left[0, :, rows], right[f * count, :, cols])
                for s in range(1, count):
                    v = v + tn(left[s, :, rows], right[f * count + s, :, cols])
                if form == "f":
                    out[f, rows, cols] = v
                elif form == "x":
                    here = slice(t * LANE, (t + 1) * LANE)
                    out[2 * f, here, cols] = v[LANE:, :].astype(BF16)
                    out[2 * f + 1, here, cols] = v[:LANE, :].astype(BF16)
                else:
                    out[2 * f + 1 - t, :, cols] = v.astype(BF16)
            for i in range(per * f, per * (f + 1)):
                done += move.start(out.at[i, :, cols], outs[i].at[:, cols])
    wait(done)


def grad_call(perm, lefts, rights, keeps, col, count, forms):
    rows, width = lefts[0].shape
    full = forms[0] == "f"
    height = width if full else width // 2
    outs = ([sds((height, count), F32)] if full else [sds((height // 2, count), BF16)] * 2) * len(forms)
    parts = len(chunks(count))
    return call(
        functools.partial(grad_body, bool(keeps), forms, col),
        perm,
        keeps,
        [*lefts, *(r for group in rights for r in group)],
        outs,
        [
            pltpu.VMEM((len(lefts), rows, height), BF16),
            pltpu.VMEM((len(lefts) * len(forms), rows, count), BF16),
            pltpu.VMEM((len(outs), outs[0].shape[0], count), outs[0].dtype),
        ],
        len(lefts) * (height // LANE + parts * len(forms)) + len(outs) * parts,
        "grad_" + "".join(forms),
    )


def rotary_tables(positions):
    half = HEAD // 2
    exponent = jnp.arange(half, dtype=F32) * (2.0 / HEAD)
    frequency = jnp.exp(-exponent * math.log(rope_base))
    angles = positions.astype(F32)[:, None] * frequency[None, :]
    cos, sin = jnp.cos(angles), jnp.sin(angles)
    return jnp.concatenate([cos, cos, cos, cos], axis=-1), jnp.concatenate([-sin, sin, -sin, sin], axis=-1)


def on_device(tokens, segments, cotangent, attn_gain, w_qkv, w_attn_out, mlp_gain, w_in, w_mlp_out):
    micro_count, seq_count, local_len, width = tokens.shape
    hidden = w_mlp_out.shape[1]
    padded = -(-hidden // LANE) * LANE
    dp_count = lax.axis_size("dp")
    ctx_count = lax.axis_size("ctx")
    part = width // (dp_count * ctx_count)
    blocks = width // LANE
    half_len = local_len // 2
    rows = ctx_count * half_len
    assert seq_count == 1 and ctx_count == 2 * micro_count and dp_count % 2 == 0
    fast = dp_count == 8 and ctx_count * part == LANE
    dp = lax.axis_index("dp")
    low = dp % 2

    def swap(v, bit):
        return lax.ppermute(v, "dp", [(i, i ^ bit) for i in range(dp_count)])

    def tie(v, *after):
        return lax.optimization_barrier((v, *after))[0] if after else v

    def across(v):
        return lax.all_to_all(v, "ctx", split_axis=0, concat_axis=0, tiled=True)

    def pick(zero, one):
        return jnp.where(low == 0, zero, one)

    def spread(shard):
        return jnp.broadcast_to(shard[None], (ctx_count, *shard.shape))

    def flat(v):
        return v.reshape(v.shape[0] * v.shape[1], v.shape[2])

    def halves_out(v):
        halves = v.reshape(micro_count, 2, half_len, width)
        return pick(halves[:, 0], halves[:, 1]), pick(halves[:, 1], halves[:, 0])

    def join_in(mine, other):
        both = jnp.stack([pick(mine, other), pick(other, mine)], axis=1)
        return both.reshape(ctx_count, half_len, width)

    def split_back(got):
        got = got.reshape(micro_count, 2, half_len, width)
        return pick(got[:, 0], got[:, 1]), pick(got[:, 1], got[:, 0])

    def join_back(mine, other):
        both = jnp.stack([pick(mine, other), pick(other, mine)], axis=1)
        return both.reshape(micro_count, 1, local_len, width)

    step = jnp.arange(rows, dtype=jnp.int32)
    positions = step // half_len * local_len + low * half_len + step % half_len
    cos, sin = rotary_tables(positions)

    index = jnp.arange(blocks, dtype=jnp.int32)
    if fast:
        turned = (index // 4) + 4 * (index // 2 % 2) + 2 * (index % 2)
        perm = jnp.bitwise_xor(turned, dp.astype(jnp.int32))
    else:
        perm = index

    third = 3 * width // 2
    seg = segments.reshape(micro_count, local_len)
    seg_cols = micro_count * local_len // part
    gain_cols = jnp.concatenate(
        [
            attn_gain[:, None],
            mlp_gain[:, None],
            seg.astype(BF16).reshape(part, seg_cols) if fast else jnp.zeros((part, 0), BF16),
            jnp.zeros((part, LANE - 2 - (seg_cols if fast else 0)), BF16),
        ],
        axis=1,
    )
    pad = ((0, 0), (0, padded - hidden))
    first_cols = third + LANE
    hw = width // 2
    thirds = [w_qkv[:, i * hw : (i + 1) * hw] for i in range(6)]
    shard_qkv = jnp.concatenate(thirds[0::2] + [gain_cols] + thirds[1::2], axis=1)
    shard_rest = jnp.concatenate([w_attn_out, jnp.pad(w_in[:, :hidden], pad), jnp.pad(w_in[:, hidden:], pad)], axis=1)
    shard_down = jnp.pad(w_mlp_out, pad)
    cut = (width + 2 * padded) // 2 // LANE * LANE

    def gather_all(shard):
        return lax.all_gather(shard, ("dp", "ctx"), axis=0, tiled=True)

    def gather_line(shard):
        return lax.all_gather(shard, "ctx", axis=0, tiled=True)

    last = []

    def order(v, *after):
        return tie(v, *last, *after)

    def did(out):
        last[:] = [jax.tree.leaves(out)[0]]
        return out

    mine, other = halves_out(tokens)
    cot_mine, cot_other = halves_out(cotangent)
    live = {}

    def sync(**more):
        live.update(more)
        names, leaves = zip(*live.items())
        live.update(zip(names, lax.optimization_barrier(leaves)))
        return [live[k] for k in more]

    if fast:
        other = swap(other, 1)
        own1 = gather_line(shard_qkv)
        a1, b1, other, mine = sync(a1=own1[:, :first_cols], b1=own1[:, first_cols:], other=other, mine=mine)
        (rest_in,) = sync(rest_in=shard_rest)
        own2 = gather_line(rest_in)
        sync(cos=cos, sin=sin, perm=perm, down_in=spread(shard_down))
        xa1, yb1, ca1, cb1 = sync(xa1=swap(a1, 2), yb1=swap(b1, 4), ca1=swap(a1, 1), cb1=swap(b1, 1))
        a1, b1 = live["a1"], live["b1"]
        sync(ya1=swap(a1, 4), yxa1=swap(xa1, 4), xb1=swap(b1, 2), xyb1=swap(yb1, 2), cxa1=swap(xa1, 1), cyb1=swap(yb1, 1))
        sync(own2=own2, **{"c" + k: swap(live[k], 1) for k in ("ya1", "yxa1", "xb1", "xyb1")})
        a2, b2 = live["own2"][:, :cut], live["own2"][:, cut:]
        x_in = across(join_in(live["mine"], live["other"]))
        cot_other = swap(tie(cot_other, live["own2"]), 1)
        sync(cot_other=cot_other, cot_mine=cot_mine, xa2=swap(a2, 2), yb2=swap(b2, 4), x_in=x_in, a2=a2, b2=b2)
        qkv0 = [live[k] for k in ("a1", "xa1", "ya1", "yxa1", "ca1", "cxa1", "cya1", "cyxa1")]
        qkv1 = [live[k] for k in ("b1", "xb1", "yb1", "xyb1", "cb1", "cxb1", "cyb1", "cxyb1")]
        cos, sin, perm = live["cos"], live["sin"], live["perm"]
        x = flat(live["x_in"])
        seg_at = slice(third + 2, third + 2 + seg_cols)
        z = lax.axis_index("ctx")
        seg_from = jnp.where(z % 2 == low, qkv0[0][:, seg_at], qkv0[4][:, seg_at])
        seg_from = seg_from.reshape(ctx_count, micro_count, local_len)
        seg_all = lax.dynamic_index_in_dim(seg_from, z // 2, 1, False).astype(jnp.int32)
    else:
        qkv0, qkv1 = [gather_all(shard_qkv[:, :first_cols])], [gather_all(shard_qkv[:, first_cols:])]
        rest_a, rest_b = [gather_all(shard_rest[:, :cut])], [gather_all(shard_rest[:, cut:])]
        wdown = [gather_all(shard_down)]
        x = flat(across(join_in(mine, swap(other, 1))))
        cot = flat(across(join_in(cot_mine, swap(cot_other, 1))))
        seg_other = swap(seg, 1)
        seg_all = across(jnp.stack([pick(seg, seg_other), pick(seg_other, seg)], axis=1).reshape(ctx_count, local_len))

    seg_halves = seg_all.reshape(ctx_count, 2, half_len)
    seg_mine = pick(seg_halves[:, 0], seg_halves[:, 1]).reshape(rows)
    seg_theirs = pick(seg_halves[:, 1], seg_halves[:, 0]).reshape(rows)
    segq = seg_mine.reshape(1, rows)
    wide = lambda v: jnp.broadcast_to(v[:, None], (v.shape[0], LANE))
    segk = wide(jnp.concatenate([seg_mine, seg_theirs]))
    keep, keep_theirs = wide((seg_mine != 0).astype(F32)), wide((seg_theirs != 0).astype(F32))

    attn_in, q, kv, gains = qkv_call(perm, x, cos, sin, qkv0, qkv1)
    part_one = blocks // 2
    if fast:
        own3 = flat(across(live["down_in"]))
        sync(
            attn_in=attn_in, q=q, kv=kv, gains=gains, segq=segq, segk=segk, keep=keep,
            keep_theirs=keep_theirs, own3=own3, ya2=swap(live["a2"], 4), xb2=swap(live["b2"], 2),
            ca2=swap(live["a2"], 1), cb2=swap(live["b2"], 1), cot_in=join_in(live["cot_mine"], live["cot_other"]),
        )
        cot_in = live.pop("cot_in")
        attn_in, q, kv, gains = (live[k] for k in ("attn_in", "q", "kv", "gains"))
        segq, segk, perm = live["segq"], live["segk"], live["perm"]
    kv_other = swap(kv, 1)
    oa, pa = attend_call(perm, segk, segq, q, kv, kv_other, 0, part_one)
    oa_first = oa
    if fast:
        sync(kv_other=kv_other, yxa2=swap(live["xa2"], 4), xyb2=swap(live["yb2"], 2), oa=oa, **{"c" + k: swap(live[k], 1) for k in ("xa2", "yb2")})
        oa = live["oa"]
        attn_in, q, kv, gains, kv_other = (live[k] for k in ("attn_in", "q", "kv", "gains", "kv_other"))
        segq, segk, perm = live["segq"], live["segk"], live["perm"]
    ob, pb = attend_call(perm, segk, segq, q, kv, kv_other, part_one, blocks - part_one)
    if fast:
        cores = {"c" + k: swap(live[k], 1) for k in ("ya2", "xb2", "yxa2")}
        cot = flat(across(tie(cot_in, oa_first)))
        sync(ob=ob, xd=swap(live["own3"], 2), yd=swap(live["own3"], 4), x=x, **cores)
        rest_a = [live[k] for k in ("a2", "xa2", "ya2", "yxa2", "ca2", "cxa2", "cya2", "cyxa2")]
        rest_b = [live[k] for k in ("b2", "xb2", "yb2", "xyb2", "cb2", "cxb2", "cyb2")]
        rest_b.append(swap(live["xyb2"], 1))
        attn_in, q, kv, gains, kv_other, x = (live[k] for k in ("attn_in", "q", "kv", "gains", "kv_other", "x"))
        perm, oa, ob = live["perm"], live["oa"], live["ob"]
        keep, keep_theirs = live["keep"], live["keep_theirs"]
        own3, xd, yd = live["own3"], live["xd"], live["yd"]
        xyd = swap(yd, 2)
        cores = [swap(v, 1) for v in (own3, xd, yd)]

    def pair(v, *after):
        return (v, swap(tie(v, *after), 1) if fast else None)

    h1, mlp_in, attended = middle_call(perm, gains, x, keep, oa, ob, rest_a)
    mixed, f1, f2 = gate_call(perm, mlp_in, rest_a, rest_b, padded, width, cut)
    if fast:
        attended, h1, mlp_in, mixed, f1, f2, cot, xyd, *cores = sync(
            attended=attended, h1=h1, mlp_in=mlp_in, mixed=mixed, f1=f1, f2=f2, cot=cot, xyd=xyd,
            **{"cores%d" % i: v for i, v in enumerate(cores)},
        )
        attn_in, gains, x, keep, perm = (live[k] for k in ("attn_in", "gains", "x", "keep", "perm"))
        own3, xd, yd = (live[k] for k in ("own3", "xd", "yd"))
        wdown = [own3, xd, yd, xyd, *cores, swap(xyd, 1)]
        others = [swap(tie(v, wdown[-1]), 1) for v in (mixed, cot, mlp_in, attn_in, attended)]
    dgate, dup, rows_out = did(dgate_call(perm, cot, keep, f1, f2, h1, mixed, wdown))
    if fast:
        dgate, dup, rows_out, mixed_other, cot_other, mlp_other, a_other, o_other = sync(
            dgate=dgate, dup=dup, rows_out=rows_out, **{"other%d" % i: v for i, v in enumerate(others)}
        )
        perm, cot, mixed, keep, keep_theirs, mlp_in = (
            live[k] for k in ("perm", "cot", "mixed", "keep", "keep_theirs", "mlp_in")
        )
        cot_pair, mixed_pair, mlp_pair = (cot, cot_other), (mixed, mixed_other), (mlp_in, mlp_other)
        in_pair, o_pair = (attn_in, a_other), (attended, o_other)
    else:
        cot_pair, mixed_pair, mlp_pair, in_pair, o_pair = ((v, None) for v in (cot, mixed, mlp_in, attn_in, attended))
    dgate_pair, dup_pair = pair(dgate), pair(dup)

    class Reduce:
        def __init__(self, count, form, grads):
            self.count = count
            if not fast:
                self.out = lax.psum_scatter(grads[0], ("dp", "ctx"), scatter_dimension=0, tiled=True)
                return
            leave, self.kept = grads
            first, self.second = (2, 4) if form == "x" else (4, 2)
            self.half = leave.shape[0] // 2
            self.got = swap(leave, first)

        def two(self):
            if fast:
                h = self.half
                kept = order(self.kept)
                leave = did((kept[h:].astype(F32) + self.got[h:].astype(F32)).astype(BF16))
                self.got2 = swap(leave, self.second)

        def three(self):
            got2 = order(self.got2)
            h = self.half
            total = self.kept[:h].astype(F32) + self.got[:h].astype(F32) + got2.astype(F32)
            return did(total.astype(BF16))

    def finish(first, *some):
        return tie(first, *(r.out for r in some)) if fast else first

    def reductions(left, rights, keeps, col, count, forms, tied=None):
        if not fast:
            got = [did(grad_call(order(perm), left[:1], [r[:1]], keeps[:1], col, count, ("f",))) for r in rights]
            return [Reduce(count, None, g) for g in got]
        got = did(grad_call(order(perm) if tied is None else tied, left, rights, keeps, col, count, forms))
        return [Reduce(count, form, got[2 * i : 2 * i + 2]) for i, form in enumerate(forms)]

    def line(*some):
        if fast:
            totals = [r.three() for r in some]
            total = did(jnp.concatenate(totals, axis=1)) if len(some) > 1 else totals[0]
            total = lax.psum_scatter(total, "ctx", scatter_dimension=0, tiled=True).astype(F32)
            at = 0
            for r in some:
                r.out = total[:, at : at + r.count]
                at += r.count

    out_got = across(rows_out.reshape(ctx_count, half_len, width))
    (r_down,) = reductions(cot_pair, [mixed_pair], [keep, keep_theirs], 0, padded, ("x",))
    r_gate, r_up = reductions(mlp_pair, [dgate_pair, dup_pair], [], 0, padded, ("y", "x"))
    dh1, e_attn, d_o, gain_two = did(dmiddle_call(order(perm), gains, cot, keep, h1, dgate, dup, rest_a, rest_b, width, cut))
    e_pair = pair(e_attn)
    r_down.two()
    (r_out,) = reductions(o_pair, [e_pair], [], 0, width, ("y",))

    tied, out_got = lax.optimization_barrier((order(perm), out_got))
    dq, dk0, dv0, dk1, dv1 = did(dattend_call(tied, q, kv, kv_other, d_o, pa, 0))
    dk_got, dv_got = swap(dk1, 1), swap(dv1, 1)
    r_gate.two()
    da = did(dqkv_call(order(perm), cos, sin, dq, dk0, dv0, dk_got, dv_got))
    da_pair = pair(da)
    r_up.two()
    line(r_down)
    (r_qkva,) = reductions(in_pair, [da_pair], [], 0, third, ("y",))
    dq, dk0, dv0, dk1, dv1 = did(dattend_call(order(perm), q, kv, kv_other, d_o, pb, part_one))
    dk_got, dv_got = swap(dk1, 1), swap(dv1, 1)
    r_out.two()
    line(r_gate)
    db = did(dqkv_call(finish(order(perm), r_down), cos, sin, dq, dk0, dv0, dk_got, dv_got))
    db_pair = pair(db)
    line(r_up, r_out)
    input_rows, gain_one = did(dinput_call(order(perm), gains, x, dh1, da, db, qkv0, qkv1))
    in_got = across(input_rows.reshape(ctx_count, half_len, width))
    sub = third // 2
    gain_rows = jnp.concatenate([gain_one, gain_two], axis=0)
    if fast:
        gain_got = swap(gain_rows, 2)
    (r_qkvb0,) = reductions(in_pair, [db_pair], [], 0, sub, ("x",), finish(order(perm), r_gate))
    if fast:
        gain_rows = did(order(gain_rows) + gain_got)
        gain_got = swap(gain_rows, 4)
    (r_qkvb1,) = reductions(in_pair, [db_pair], [], sub, sub, ("y",))
    r_qkva.two()
    if fast:
        gain_rows = did(order(gain_rows) + gain_got)
        gain_got = swap(gain_rows, 1)
        r_qkvb0.kept = finish(r_qkvb0.kept, r_up)
    r_qkvb0.two()
    if fast:
        r_qkvb0.got2 = tie(r_qkvb0.got2, in_got)
    r_qkvb1.two()
    line(r_qkva, r_qkvb0, r_qkvb1)
    out_mine, out_other = split_back(out_got)
    layer_out = join_back(out_mine, swap(out_other, 1))
    if fast:
        gain_rows = gain_rows + gain_got
        for bit in (1, 2):
            gain_rows = gain_rows + lax.ppermute(gain_rows, "ctx", [(i, i ^ bit) for i in range(ctx_count)])
        gain_grads = lax.dynamic_slice(gain_rows, (0, (dp * ctx_count + lax.axis_index("ctx")) * part), (2, part))
    else:
        gain_grads = lax.psum_scatter(gain_rows, ("dp", "ctx"), scatter_dimension=1, tiled=True)
    qkvb = jnp.concatenate([r_qkvb0.out, r_qkvb1.out], axis=1)
    qkv_grad = jnp.concatenate(
        [half[:, i * hw : (i + 1) * hw] for i in range(3) for half in (r_qkva.out, qkvb)], axis=1
    )
    in_mine, in_other = split_back(in_got)
    input_grad = join_back(in_mine, swap(in_other, 1))

    return (
        layer_out,
        input_grad,
        gain_grads[0],
        qkv_grad,
        r_out.out,
        gain_grads[1],
        jnp.concatenate([r_gate.out[:, :hidden], r_up.out[:, :hidden]], axis=1),
        r_down.out[:, :hidden],
    )


def solution(mesh):
    return jax.shard_map(
        on_device,
        mesh=mesh,
        in_specs=(
            P(None, "dp", "ctx", None),
            P(None, "dp", "ctx"),
            P(None, "dp", "ctx", None),
            P(("dp", "ctx")),
            P(("dp", "ctx"), None),
            P(("dp", "ctx"), None),
            P(("dp", "ctx")),
            P(("dp", "ctx"), None),
            P(("dp", "ctx"), None),
        ),
        out_specs=(
            P(None, "dp", "ctx", None),
            P(None, "dp", "ctx", None),
            P(("dp", "ctx")),
            P(("dp", "ctx"), None),
            P(("dp", "ctx"), None),
            P(("dp", "ctx")),
            P(("dp", "ctx"), None),
            P(("dp", "ctx"), None),
        ),
        check_vma=False,
    )
```

profile of v0, /device:TPU:0, one launch (start us, length us, event | category | flops | bytes accessed | tf_op | source)
XLA Modules:
  0.0 425.0 jit_solution(11577614180909325098)
XLA Ops:
  9.6 21.3 %all_gather.6 = bf16[128,3200]{1,0:T(8,128)(2,1)S(1)} all-gather(bf16[32,3200]{1,0:T(8,128)(2,1)S(1)} %concatenate.31), channel_id=1, replica_groups=mesh['dp'=8,'ctx'=4] {'ctx'}, dimensions={0}, use_global_device_ids=true | all-gather | bytes 1024000 | tf_op jit(solution)/shard_map/all_gather | solution.py:853
  48.6 6.2 %collective-permute-done.7.rest_9_ = bf16[128,1536]{1,0:T(8,128)(2,1)S(1)} collective-permute-done((bf16[128,1536]{1,0:T(8,128)(2,1)S(1)}, bf16[128,1536]{1,0:T(8,128)(2,1)S(1)}, u32[]{:S(2)}, u32[]{:S(2)}) %collective-permute-start.7) | collective-permute-done | bytes 393248 | tf_op jit(solution)/shard_map/ppermute | solution.py:784
  54.8 6.2 %collective-permute-done.8.rest_11_ = bf16[128,1536]{1,0:T(8,128)(2,1)S(1)} collective-permute-done((bf16[128,1536]{1,0:T(8,128)(2,1)S(1)}, bf16[128,1536]{1,0:T(8,128)(2,1)S(1)}, u32[]{:S(2)}, u32[]{:S(2)}) %collective-permute-start.8) | collective-permute-done | bytes 393248 | tf_op jit(solution)/shard_map/ppermute | solution.py:784
  85.2 13.7 %collective-permute-done.16.rest_1_ = bf16[128,3200]{1,0:T(8,128)(2,1)S(1)} collective-permute-done((bf16[128,3200]{1,0:T(8,128)(2,1)S(1)}, bf16[128,3200]{1,0:T(8,128)(2,1)S(1)}, u32[]{:S(2)}, u32[]{:S(2)}) %collective-permute-start.16) | collective-permute-done | bytes 819232 | tf_op jit(solution)/shard_map/ppermute | solution.py:784
  113.0 11.4 %qkv.1 = (bf16[512,1024]{1,0:T(8,128)(2,1)}, bf16[512,1024]{1,0:T(8,128)(2,1)}, bf16[512,2048]{1,0:T(8,128)(2,1)}, f32[8,1024]{1,0:T(8,128)}) custom-call(s32[8]{0:T(128)} %fusion.20.perm, f32[512,128]{1,0:T(8,128)} %get-tuple-element.371.cos_ref, f32[512,128]{1,0:T(8,128)} %get-tuple-element.372.sin_ref, bf16[512,1024]{1,0:T(8,128)(2,1)} %bitcast.136, ...), custom_call_target="tpu_custom_call" | custom-call | flops 1 | bytes 1 | tf_op jit(solution)/shard_map/qkv/pallas_call | solution.py:96
  136.8 12.0 %attend.2 = (bf16[512,512]{1,0:T(8,128)(2,1)}, bf16[4,2,1024,512]{3,2,1,0:T(8,128)(2,1)}) custom-call(s32[8]{0:T(128)} %fusion.20.perm, s32[1024,128]{1,0:T(8,128)} %broadcast_in_dim.18.segk_ref, s32[1,512]{1,0:T(1,128)} %bitcast.154, bf16[512,1024]{1,0:T(8,128)(2,1)} %get-tuple-element.450.q_ref, bf16[512,2048]{1,0:T(8,128)(2,1)} %get-tuple-element.451.k0_ref.v0_ref, ...), custom_call_target="tpu_custom_call" | custom-call | flops 1 | bytes 1 | tf_op jit(solution)/shard_map/attend/pallas_call | solution.py:228
  159.6 12.3 %attend.3 = (bf16[512,512]{1,0:T(8,128)(2,1)}, bf16[4,2,1024,512]{3,2,1,0:T(8,128)(2,1)}) custom-call(s32[8]{0:T(128)} %fusion.20.perm, s32[1024,128]{1,0:T(8,128)} %broadcast_in_dim.18.segk_ref, s32[1,512]{1,0:T(1,128)} %bitcast.155, bf16[512,1024]{1,0:T(8,128)(2,1)} %get-tuple-element.450.q_ref, bf16[512,2048]{1,0:T(8,128)(2,1)} %get-tuple-element.451.k0_ref.v0_ref, ...), custom_call_target="tpu_custom_call" | custom-call | flops 1 | bytes 1 | tf_op jit(solution)/shard_map/attend/pallas_call | solution.py:228
  178.0 6.3 %middle.1 = (f32[512,1024]{1,0:T(8,128)}, bf16[512,1024]{1,0:T(8,128)(2,1)}, bf16[512,1024]{1,0:T(8,128)(2,1)}) custom-call(s32[8]{0:T(128)} %fusion.20.perm, f32[8,1024]{1,0:T(8,128)} %get-tuple-element.483.gains_ref, f32[512,128]{1,0:T(8,128)} %broadcast_in_dim.19.keep_ref.refs_0_, bf16[512,1024]{1,0:T(8,128)(2,1)} %bitcast.137, ...), custom_call_target="tpu_custom_call" | custom-call | flops 1 | bytes 1 | tf_op jit(solution)/shard_map/middle/pallas_call | solution.py:96
  185.2 11.8 %gate.1 = (bf16[512,2688]{1,0:T(8,128)(2,1)}, bf16[512,2688]{1,0:T(8,128)(2,1)}, bf16[512,2688]{1,0:T(8,128)(2,1)}) custom-call(s32[8]{0:T(128)} %fusion.20.perm, bf16[512,1024]{1,0:T(8,128)(2,1)} %get-tuple-element.520.b_hbm.refs_0_, bf16[128,3200]{1,0:T(8,128)(2,1)} %copy-done.4, bf16[128,3200]{1,0:T(8,128)(2,1)} %copy-done.7, ...), custom_call_target="tpu_custom_call" | custom-call | flops 1 | bytes 1 | tf_op jit(solution)/shard_map/gate/pallas_call | solution.py:96
  201.9 13.0 %dgate.1 = (bf16[512,2688]{1,0:T(8,128)(2,1)}, bf16[512,2688]{1,0:T(8,128)(2,1)}, bf16[512,1024]{1,0:T(8,128)(2,1)}) custom-call(s32[8]{0:T(128)} %fusion.20.perm, f32[512,128]{1,0:T(8,128)} %broadcast_in_dim.19.keep_ref.refs_0_, bf16[512,1024]{1,0:T(8,128)(2,1)} %bitcast.140, bf16[512,2688]{1,0:T(8,128)(2,1)} %get-tuple-element.494.f1_hbm, ...), custom_call_target="tpu_custom_call" | custom-call | flops 1 | bytes 1 | tf_op jit(solution)/shard_map/dgate/pallas_call | solution.py:96
  216.5 7.7 %grad_x.2 = (bf16[256,2688]{1,0:T(8,128)(2,1)}, bf16[256,2688]{1,0:T(8,128)(2,1)}) custom-call(s32[8]{0:T(128)} %fusion.20.perm, f32[512,128]{1,0:T(8,128)} %broadcast_in_dim.19.keep_ref.refs_0_, f32[512,128]{1,0:T(8,128)} %broadcast_in_dim.20.refs_1_, bf16[512,1024]{1,0:T(8,128)(2,1)} %bitcast.141, bf16[512,1024]{1,0:T(8,128)(2,1)} %collective-permute-done.39.refs_3_, ...), custom_call_target="tpu_custom_call" | custom-call | flops 1 | bytes 1 | tf_op jit(solution)/shard_map/grad_x/pallas_call | solution.py:96
  224.8 4.7 %all-to-all-start.3 = ((bf16[4,128,1024]{2,1,0:T(8,128)(2,1)}), bf16[4,128,1024]{2,1,0:T(8,128)(2,1)S(1)}, u32[]{:S(2)}, u32[]{:S(2)}) async-start(bf16[4,128,1024]{2,1,0:T(8,128)(2,1)} %bitcast.21), calls=%async_computation.3 | async-start | bytes 2097152 | tf_op jit(solution)/shard_map/all_to_all | solution.py:790
  229.6 11.0 %grad_yx.1 = (bf16[256,2688]{1,0:T(8,128)(2,1)}, bf16[256,2688]{1,0:T(8,128)(2,1)}, bf16[256,2688]{1,0:T(8,128)(2,1)}, bf16[256,2688]{1,0:T(8,128)(2,1)}) custom-call(s32[8]{0:T(128)} %fusion.20.perm, bf16[512,1024]{1,0:T(8,128)(2,1)} %get-tuple-element.520.b_hbm.refs_0_, bf16[512,1024]{1,0:T(8,128)(2,1)} %collective-permute-done.40.refs_1_, ...), custom_call_target="tpu_custom_call" | custom-call | flops 1 | bytes 1 | tf_op jit(solution)/shard_map/grad_yx/pallas_call | solution.py:96
  242.1 15.0 %dmiddle.1 = (f32[512,1024]{1,0:T(8,128)}, bf16[512,1024]{1,0:T(8,128)(2,1)}, bf16[512,1024]{1,0:T(8,128)(2,1)}, f32[1,1024]{1,0:T(1,128)}) custom-call(s32[8]{0:T(128)} %fusion.20.perm, f32[8,1024]{1,0:T(8,128)} %get-tuple-element.483.gains_ref, f32[512,128]{1,0:T(8,128)} %broadcast_in_dim.19.keep_ref.refs_0_, bf16[512,1024]{1,0:T(8,128)(2,1)} %bitcast.142, ...), custom_call_target="tpu_custom_call" | custom-call | flops 1 | bytes 1 | tf_op jit(solution)/shard_map/dmiddle/pallas_call | solution.py:96
  262.3 5.0 %grad_y.3 = (bf16[256,1024]{1,0:T(8,128)(2,1)}, bf16[256,1024]{1,0:T(8,128)(2,1)}) custom-call(s32[8]{0:T(128)} %fusion.20.perm, bf16[512,1024]{1,0:T(8,128)(2,1)} %get-tuple-element.508.refs_0_, bf16[512,1024]{1,0:T(8,128)(2,1)} %collective-permute-done.42.refs_1_, bf16[512,1024]{1,0:T(8,128)(2,1)} %get-tuple-element.530.refs_2_, bf16[512,1024]{1,0:T(8,128)(2,1)} %copy-done.42), custom_call_target="tpu_custom_call" | custom-call | flops 1 | bytes 1 | tf_op jit(solution)/shard_map/grad_y/pallas_call | solution.py:96
  268.9 14.2 %dattend.2 = (bf16[512,512]{1,0:T(8,128)(2,1)}, f32[512,512]{1,0:T(8,128)}, f32[512,512]{1,0:T(8,128)}, bf16[512,512]{1,0:T(8,128)(2,1)}, bf16[512,512]{1,0:T(8,128)(2,1)}) custom-call(s32[8]{0:T(128)} %fusion.20.perm, bf16[512,1024]{1,0:T(8,128)(2,1)} %get-tuple-element.450.q_ref, bf16[512,2048]{1,0:T(8,128)(2,1)} %get-tuple-element.451.k0_ref.v0_ref, ...), custom_call_target="tpu_custom_call" | custom-call | flops 1 | bytes 1 | tf_op jit(solution)/shard_map/dattend/pallas_call | solution.py:564
  298.4 5.7 %grad_y.4 = (bf16[256,1536]{1,0:T(8,128)(2,1)}, bf16[256,1536]{1,0:T(8,128)(2,1)}) custom-call(s32[8]{0:T(128)} %fusion.20.perm, bf16[512,1024]{1,0:T(8,128)(2,1)} %get-tuple-element.507.refs_0_, bf16[512,1024]{1,0:T(8,128)(2,1)} %copy-done.6, bf16[512,1536]{1,0:T(8,128)(2,1)} %dqkv.2.refs_2_.da_hbm, bf16[512,1536]{1,0:T(8,128)(2,1)} %copy-done.33), custom_call_target="tpu_custom_call" | custom-call | flops 1 | bytes 1 | tf_op jit(solution)/shard_map/grad_y/pallas_call | solution.py:96
  304.1 14.5 %dattend.3 = (bf16[512,512]{1,0:T(8,128)(2,1)}, f32[512,512]{1,0:T(8,128)}, f32[512,512]{1,0:T(8,128)}, bf16[512,512]{1,0:T(8,128)(2,1)}, bf16[512,512]{1,0:T(8,128)(2,1)}) custom-call(s32[8]{0:T(128)} %fusion.20.perm, bf16[512,1024]{1,0:T(8,128)(2,1)} %get-tuple-element.450.q_ref, bf16[512,2048]{1,0:T(8,128)(2,1)} %get-tuple-element.451.k0_ref.v0_ref, ...), custom_call_target="tpu_custom_call" | custom-call | flops 1 | bytes 1 | tf_op jit(solution)/shard_map/dattend/pallas_call | solution.py:564
  333.5 9.2 %dinput.1 = (bf16[512,1024]{1,0:T(8,128)(2,1)}, f32[1,1024]{1,0:T(1,128)}) custom-call(s32[8]{0:T(128)} %fusion.20.perm, f32[8,1024]{1,0:T(8,128)} %get-tuple-element.483.gains_ref, bf16[512,1024]{1,0:T(8,128)(2,1)} %bitcast.138, f32[512,1024]{1,0:T(8,128)} %get-tuple-element.526.dh1_hbm, bf16[512,1536]{1,0:T(8,128)(2,1)} %dqkv.2.refs_2_.da_hbm, ...), custom_call_target="tpu_custom_call" | custom-call | flops 1 | bytes 1 | tf_op jit(solution)/shard_map/dinput/pallas_call | solution.py:96
  344.3 5.2 %all-to-all-start.4 = ((bf16[4,128,1024]{2,1,0:T(8,128)(2,1)}), bf16[4,128,1024]{2,1,0:T(8,128)(2,1)S(1)}, u32[]{:S(2)}, u32[]{:S(2)}) async-start(bf16[4,128,1024]{2,1,0:T(8,128)(2,1)} %bitcast.150), calls=%async_computation.5 | async-start | bytes 2097152 | tf_op jit(solution)/shard_map/all_to_all | solution.py:790
  349.5 4.5 %grad_x.3 = (bf16[256,768]{1,0:T(8,128)(2,1)}, bf16[256,768]{1,0:T(8,128)(2,1)}) custom-call(s32[8]{0:T(128)} %fusion.20.perm, bf16[512,1024]{1,0:T(8,128)(2,1)} %get-tuple-element.507.refs_0_, bf16[512,1024]{1,0:T(8,128)(2,1)} %copy-done.6, bf16[512,1536]{1,0:T(8,128)(2,1)} %dqkv.3.db_hbm.refs_2_, bf16[512,1536]{1,0:T(8,128)(2,1)} %collective-permute-done.61.refs_3_), custom_call_target="tpu_custom_call" | custom-call | flops 1 | bytes 1 | tf_op jit(solution)/shard_map/grad_x/pallas_call | solution.py:96
  375.5 4.8 %collective-permute-done.68 = bf16[128,1536]{1,0:T(8,128)(2,1)S(1)} collective-permute-done((bf16[128,1536]{1,0:T(8,128)(2,1)S(1)}, bf16[128,1536]{1,0:T(8,128)(2,1)S(1)}, u32[]{:S(2)}, u32[]{:S(2)}) %collective-permute-start.68) | collective-permute-done | bytes 393248 | tf_op jit(solution)/shard_map/ppermute | solution.py:784
  386.8 5.1 %reduce-scatter.11.cloned.1.call-done = bf16[32,3712]{1,0:T(8,128)(2,1)} async-done(((bf16[128,3712]{1,0:T(8,128)(2,1)}), bf16[32,3712]{1,0:T(8,128)(2,1)}) %reduce-scatter.11.cloned.1.call-update) | async-done | bytes 237584 | tf_op jit(solution)/shard_map/reduce_scatter | solution.py:1016
  396.5 20.0 %reduce-scatter.9.cloned.1.call-done = bf16[32,3072]{1,0:T(8,128)(2,1)} async-done(((bf16[128,3072]{1,0:T(8,128)(2,1)}), bf16[32,3072]{1,0:T(8,128)(2,1)}) %reduce-scatter.9.cloned.1.call-update) | async-done | bytes 196624 | tf_op jit(solution)/shard_map/reduce_scatter | solution.py:1016
  (397 shorter events, 169.2 us)
Async XLA Ops:
  7.2 63.4 %all-gather.2.cloned.1.call-start = ((), (), s32[]{:S(2)}) async-start(), calls=%async_computation.9 | async-start | bytes 2048000 | tf_op jit(solution)/shard_map/all_gather | solution.py:853
  8.6 23.9 %collective-permute-start = (bf16[2,128,1024]{2,1,0:T(8,128)(2,1)S(1)}, bf16[2,128,1024]{2,1,0:T(8,128)(2,1)S(1)}, u32[]{:S(2)}, u32[]{:S(2)}) collective-permute-start(bf16[2,128,1024]{2,1,0:T(8,128)(2,1)S(1)} %get-tuple-element.605), channel_id=1, source_target_pairs={{0,4},{4,0},{8,12},{12,8},{16,20},{20,16},{24,28},{28,24},{1,5},{5... | collective-permute-start | bytes 1572872 | tf_op jit(solution)/shard_map/ppermute | solution.py:784
  72.9 29.4 %all-to-all-start = ((bf16[4,128,1024]{2,1,0:T(8,128)(2,1)}), bf16[4,128,1024]{2,1,0:T(8,128)(2,1)S(1)}, u32[]{:S(2)}, u32[]{:S(2)}) async-start(bf16[4,128,1024]{2,1,0:T(8,128)(2,1)} %bitcast.10), calls=%async_computation | async-start | bytes 2097152 | tf_op jit(solution)/shard_map/all_to_all | solution.py:790
  102.4 23.4 %collective-permute-start.18 = (bf16[128,3200]{1,0:T(8,128)(2,1)S(1)}, bf16[128,3200]{1,0:T(8,128)(2,1)}, u32[]{:S(2)}, u32[]{:S(2)}) collective-permute-start(bf16[128,3200]{1,0:T(8,128)(2,1)S(1)} %get-tuple-element.447.rest_0_), channel_id=1, source_target_pairs={{0,16},{4,20},{8,24},{12,28},{16,0},{20,4},{24,8},{28,12},{1,17},{... | collective-permute-start | bytes 2457608 | tf_op jit(solution)/shard_map/ppermute | solution.py:784
  105.6 23.1 %all-to-all-start.1 = ((bf16[4,32,2688]{2,1,0:T(8,128)(2,1)}), bf16[4,32,2688]{2,1,0:T(8,128)(2,1)}, u32[]{:S(2)}, u32[]{:S(2)}) async-start(bf16[4,32,2688]{2,1,0:T(8,128)(2,1)} %broadcast_in_dim.17), calls=%async_computation.1 | async-start | bytes 1376256 | tf_op jit(solution)/shard_map/all_to_all | solution.py:790
  152.5 23.1 %collective-permute-start.29 = (bf16[128,3200]{1,0:T(8,128)(2,1)}, bf16[128,3200]{1,0:T(8,128)(2,1)S(1)}, u32[]{:S(2)}, u32[]{:S(2)}) collective-permute-start(bf16[128,3200]{1,0:T(8,128)(2,1)} %collective-permute-done.18.rest_2_), channel_id=1, source_target_pairs={{0,4},{4,0},{8,12},{12,8},{16,20},{20,16},{24,28},{28,24},{1,5},{5... | collective-permute-start | bytes 2457608 | tf_op jit(solution)/shard_map/ppermute | solution.py:784
  153.4 22.2 %collective-permute-start.30 = (bf16[128,3200]{1,0:T(8,128)(2,1)}, bf16[128,3200]{1,0:T(8,128)(2,1)}, u32[]{:S(2)}, u32[]{:S(2)}) collective-permute-start(bf16[128,3200]{1,0:T(8,128)(2,1)} %collective-permute-done.19.rest_9_), channel_id=1, source_target_pairs={{0,4},{4,0},{8,12},{12,8},{16,20},{20,16},{24,28},{28,24},{1,5},{5... | collective-permute-start | bytes 2457608 | tf_op jit(solution)/shard_map/ppermute | solution.py:784
  153.7 22.0 %collective-permute-start.31 = (bf16[128,3200]{1,0:T(8,128)(2,1)}, bf16[128,3200]{1,0:T(8,128)(2,1)S(1)}, u32[]{:S(2)}, u32[]{:S(2)}) collective-permute-start(bf16[128,3200]{1,0:T(8,128)(2,1)} %collective-permute-done.23.rest_3_), channel_id=1, source_target_pairs={{0,4},{4,0},{8,12},{12,8},{16,20},{20,16},{24,28},{28,24},{1,5},{5... | collective-permute-start | bytes 2457608 | tf_op jit(solution)/shard_map/ppermute | solution.py:784
  153.9 44.1 %all-to-all-start.2 = ((bf16[4,128,1024]{2,1,0:T(8,128)(2,1)}), bf16[4,128,1024]{2,1,0:T(8,128)(2,1)S(1)}, u32[]{:S(2)}, u32[]{:S(2)}) async-start(bf16[4,128,1024]{2,1,0:T(8,128)(2,1)} %bitcast.147), calls=%async_computation.2 | async-start | bytes 2097152 | tf_op jit(solution)/shard_map/all_to_all | solution.py:790
  224.2 34.5 %collective-permute-start.45 = (bf16[256,2688]{1,0:T(8,128)(2,1)}, bf16[256,2688]{1,0:T(8,128)(2,1)}, u32[]{:S(2)}, u32[]{:S(2)}) collective-permute-start(bf16[256,2688]{1,0:T(8,128)(2,1)} %get-tuple-element.518), channel_id=1, source_target_pairs={{0,8},{4,12},{8,0},{12,4},{16,24},{20,28},{24,16},{28,20},{1,9},{5... | collective-permute-start | bytes 4128776 | tf_op jit(solution)/shard_map/ppermute | solution.py:784
  224.8 44.1 %all-to-all-start.3 = ((bf16[4,128,1024]{2,1,0:T(8,128)(2,1)}), bf16[4,128,1024]{2,1,0:T(8,128)(2,1)S(1)}, u32[]{:S(2)}, u32[]{:S(2)}) async-start(bf16[4,128,1024]{2,1,0:T(8,128)(2,1)} %bitcast.21), calls=%async_computation.3 | async-start | bytes 2097152 | tf_op jit(solution)/shard_map/all_to_all | solution.py:790
  229.5 93.7 %reduce-scatter.5.cloned.1.call-start = ((), (), s32[]{:S(2)}) async-start(), calls=%async_computation.10 | async-start | bytes 860160 | tf_op jit(solution)/shard_map/reduce_scatter | solution.py:1016
  240.6 42.6 %collective-permute-start.49 = (bf16[256,2688]{1,0:T(8,128)(2,1)}, bf16[256,2688]{1,0:T(8,128)(2,1)S(1)}, u32[]{:S(2)}, u32[]{:S(2)}) collective-permute-start(bf16[256,2688]{1,0:T(8,128)(2,1)} %get-tuple-element.524), channel_id=1, source_target_pairs={{0,16},{4,20},{8,24},{12,28},{16,0},{20,4},{24,8},{28,12},{1,17},{... | collective-permute-start | bytes 4128776 | tf_op jit(solution)/shard_map/ppermute | solution.py:784
  257.2 33.5 %collective-permute-start.48 = (bf16[256,2688]{1,0:T(8,128)(2,1)}, bf16[256,2688]{1,0:T(8,128)(2,1)}, u32[]{:S(2)}, u32[]{:S(2)}) collective-permute-start(bf16[256,2688]{1,0:T(8,128)(2,1)} %get-tuple-element.536), channel_id=1, source_target_pairs={{0,8},{4,12},{8,0},{12,4},{16,24},{20,28},{24,16},{28,20},{1,9},{5... | collective-permute-start | bytes 4128776 | tf_op jit(solution)/shard_map/ppermute | solution.py:784
  260.8 32.1 %collective-permute-start.54 = (bf16[128,2688]{1,0:T(8,128)(2,1)}, bf16[128,2688]{1,0:T(8,128)(2,1)}, u32[]{:S(2)}, u32[]{:S(2)}) collective-permute-start(bf16[128,2688]{1,0:T(8,128)(2,1)} %add_convert_fusion.5), channel_id=1, source_target_pairs={{0,16},{4,20},{8,24},{12,28},{16,0},{20,4},{24,8},{28,12},{1,17},{... | collective-permute-start | bytes 2064392 | tf_op jit(solution)/shard_map/ppermute | solution.py:784
  267.4 51.2 %collective-permute-start.56 = (bf16[256,1024]{1,0:T(8,128)(2,1)}, bf16[256,1024]{1,0:T(8,128)(2,1)}, u32[]{:S(2)}, u32[]{:S(2)}) collective-permute-start(bf16[256,1024]{1,0:T(8,128)(2,1)} %get-tuple-element.531), channel_id=1, source_target_pairs={{0,16},{4,20},{8,24},{12,28},{16,0},{20,4},{24,8},{28,12},{1,17},{... | collective-permute-start | bytes 1572872 | tf_op jit(solution)/shard_map/ppermute | solution.py:784
  285.3 36.2 %collective-permute-start.53 = (bf16[128,2688]{1,0:T(8,128)(2,1)}, bf16[128,2688]{1,0:T(8,128)(2,1)S(1)}, u32[]{:S(2)}, u32[]{:S(2)}) collective-permute-start(bf16[128,2688]{1,0:T(8,128)(2,1)} %add_convert_fusion.4), channel_id=1, source_target_pairs={{0,8},{4,12},{8,0},{12,4},{16,24},{20,28},{24,16},{28,20},{1,9},{5... | collective-permute-start | bytes 2064392 | tf_op jit(solution)/shard_map/ppermute | solution.py:784
  295.4 54.2 %reduce-scatter.7.cloned.1.call-start = ((), (), s32[]{:S(2)}) async-start(), calls=%async_computation.11 | async-start | bytes 860160 | tf_op jit(solution)/shard_map/reduce_scatter | solution.py:1016
  296.3 66.7 %collective-permute-start.47 = (bf16[2,128,1024]{2,1,0:T(8,128)(2,1)}, bf16[2,128,1024]{2,1,0:T(8,128)(2,1)}, u32[]{:S(2)}, u32[]{:S(2)}) collective-permute-start(bf16[2,128,1024]{2,1,0:T(8,128)(2,1)} %select_bitcast_fusion.1), channel_id=1, source_target_pairs={{0,4},{4,0},{8,12},{12,8},{16,20},{20,16},{24,28},{28,24},{1,5},{5... | collective-permute-start | bytes 1572872 | tf_op jit(solution)/shard_map/ppermute | solution.py:784
  296.6 33.1 %collective-permute-start.52 = (bf16[128,2688]{1,0:T(8,128)(2,1)}, bf16[128,2688]{1,0:T(8,128)(2,1)}, u32[]{:S(2)}, u32[]{:S(2)}) collective-permute-start(bf16[128,2688]{1,0:T(8,128)(2,1)} %add_convert_fusion.3), channel_id=1, source_target_pairs={{0,16},{4,20},{8,24},{12,28},{16,0},{20,4},{24,8},{28,12},{1,17},{... | collective-permute-start | bytes 2064392 | tf_op jit(solution)/shard_map/ppermute | solution.py:784
  323.7 38.3 %collective-permute-start.63 = (bf16[256,1536]{1,0:T(8,128)(2,1)}, bf16[256,1536]{1,0:T(8,128)(2,1)S(1)}, u32[]{:S(2)}, u32[]{:S(2)}) collective-permute-start(bf16[256,1536]{1,0:T(8,128)(2,1)} %get-tuple-element.553), channel_id=1, source_target_pairs={{0,16},{4,20},{8,24},{12,28},{16,0},{20,4},{24,8},{28,12},{1,17},{... | collective-permute-start | bytes 2359304 | tf_op jit(solution)/shard_map/ppermute | solution.py:784
  344.3 39.0 %all-to-all-start.4 = ((bf16[4,128,1024]{2,1,0:T(8,128)(2,1)}), bf16[4,128,1024]{2,1,0:T(8,128)(2,1)S(1)}, u32[]{:S(2)}, u32[]{:S(2)}) async-start(bf16[4,128,1024]{2,1,0:T(8,128)(2,1)} %bitcast.150), calls=%async_computation.5 | async-start | bytes 2097152 | tf_op jit(solution)/shard_map/all_to_all | solution.py:790
  349.5 42.4 %reduce-scatter.11.cloned.1.call-start = ((), (), s32[]{:S(2)}) async-start(), calls=%async_computation.13 | async-start | bytes 1187840 | tf_op jit(solution)/shard_map/reduce_scatter | solution.py:1016
  364.1 52.4 %reduce-scatter.9.cloned.1.call-start = ((), (), s32[]{:S(2)}) async-start(), calls=%async_computation.12 | async-start | bytes 983040 | tf_op jit(solution)/shard_map/reduce_scatter | solution.py:1016
  (135 other events, 1336.8 us)
Sparse Core Ops, SparseCore 0:
  32.7 37.9 all-gather.1
  295.5 22.8 reduce-scatter.4
  323.3 23.2 reduce-scatter.6
  364.3 27.5 reduce-scatter.10
  394.1 22.3 reduce-scatter.8
where the time goes:
time: 431 us; the launch traced here: 425 us
  Pallas kernels  165 us (38%)
  waiting for transfers between devices  92.4 us (21%)
  starting transfers between devices  68.5 us (16%)
  other arithmetic  35.8 us (8%)
  local copies, waits for them, and re-layouts  26.6 us (6%)
  blocking collectives  21.3 us (5%)
  between operations  15.2 us (4%)
    pallas_call x12, Pallas kernels, call(): pl.pallas_call(body, out_shape=tuple(outs), in_specs=[SMEM] + [pl.BlockSp...  105 us
    ppermute x71, waiting for transfers between devices, swap(): return lax.ppermute(v, 'dp', [(i, i ^ bit) for i in range(dp_count)])  55.8 us
    ppermute x71, starting transfers between devices, swap(): return lax.ppermute(v, 'dp', [(i, i ^ bit) for i in range(dp_count)])  42.5 us
    pallas_call x2, Pallas kernels, dattend_call(): pl.pallas_call(dattend_body, grid=(count,), out_shape=(sds((rows, count *...  28.6 us
    reduce_scatter x4, waiting for transfers between devices, line(): lax.psum_scatter(total, 'ctx', scatter_dimension=0, tiled=True).astype(F32)  25.2 us
    pallas_call x2, Pallas kernels, attend_call(): pl.pallas_call(attend_body, grid=(count,), out_shape=(sds((rows, count *...  24.2 us
    all_to_all x5, starting transfers between devices, across(): return lax.all_to_all(v, 'ctx', split_axis=0, concat_axis=0, tiled=True)  21.3 us
    all_gather x1, blocking collectives, gather_line(): return lax.all_gather(shard, 'ctx', axis=0, tiled=True)  21.3 us
  transfers between devices with their start and end apart: 83, of which 26 were waited for; matrix products, arithmetic and copies ran while one was open for 10% of the time, Pallas kernels for 39%

commit v1 on v0

--- a/solution.py
+++ b/solution.py
@@ -1009,11 +1009,14 @@
         got = did(grad_call(order(perm) if tied is None else tied, left, rights, keeps, col, count, forms))
         return [Reduce(count, form, got[2 * i : 2 * i + 2]) for i, form in enumerate(forms)]
 
-    def line(*some):
+    def line(*some, exchange=False):
         if fast:
             totals = [r.three() for r in some]
             total = did(jnp.concatenate(totals, axis=1)) if len(some) > 1 else totals[0]
-            total = lax.psum_scatter(total, "ctx", scatter_dimension=0, tiled=True).astype(F32)
+            if exchange:
+                total = jnp.sum(across(total.reshape(ctx_count, part, total.shape[1])).astype(F32), axis=0)
+            else:
+                total = lax.psum_scatter(total, "ctx", scatter_dimension=0, tiled=True).astype(F32)
             at = 0
             for r in some:
                 r.out = total[:, at : at + r.count]
@@ -1063,7 +1066,7 @@
     if fast:
         r_qkvb0.got2 = tie(r_qkvb0.got2, in_got)
     r_qkvb1.two()
-    line(r_qkva, r_qkvb0, r_qkvb1)
+    line(r_qkva, r_qkvb0, r_qkvb1, exchange=True)
     out_mine, out_other = split_back(out_got)
     layer_out = join_back(out_mine, swap(out_other, 1))
     if fast:

time: 431 us -> 426 us (0.988)
  waiting for transfers between devices: 92.4 us -> 79.5 us
  starting transfers between devices: 68.5 us -> 73 us
    reduce_scatter x4 -> x3, waiting for transfers between devices: 25.2 us -> 0.02 us  [line(): lax.psum_scatter(total, 'ctx', scatter_dimension=0, tiled=True).astype(F32)]
    all_to_all x5 -> x6, waiting for transfers between devices: 7.68 us -> 20.3 us  [across(): return lax.all_to_all(v, 'ctx', split_axis=0, concat_axis=0, tiled=True)]
    all_to_all x5 -> x6, starting transfers between devices: 21.3 us -> 26.2 us  [across(): return lax.all_to_all(v, 'ctx', split_axis=0, concat_axis=0, tiled=True)]
    unnamed x157 -> x149, local copies, waits for them, and re-layouts: 13 us -> 13.1 us
  transfers between devices with their start and end apart: 83 -> 83, of which waited for: 26 -> 25; matrix products, arithmetic and copies ran while one was open for 10% -> 11% of each run, Pallas kernels for 39% -> 39%
where the time goes in v1:
time: 426 us; the launch traced here: 421 us
  Pallas kernels  165 us (39%)
  waiting for transfers between devices  79.5 us (19%)
  starting transfers between devices  73 us (17%)
  other arithmetic  39.5 us (9%)
  local copies, waits for them, and re-layouts  26.7 us (6%)
  blocking collectives  21.3 us (5%)
  between operations  15.2 us (4%)
    pallas_call x12, Pallas kernels, call(): pl.pallas_call(body, out_shape=tuple(outs), in_specs=[SMEM] + [pl.BlockSp...  105 us
    ppermute x71, waiting for transfers between devices, swap(): return lax.ppermute(v, 'dp', [(i, i ^ bit) for i in range(dp_count)])  55.4 us
    ppermute x71, starting transfers between devices, swap(): return lax.ppermute(v, 'dp', [(i, i ^ bit) for i in range(dp_count)])  42.2 us
    pallas_call x2, Pallas kernels, dattend_call(): pl.pallas_call(dattend_body, grid=(count,), out_shape=(sds((rows, count *...  28.9 us
    all_to_all x6, starting transfers between devices, across(): return lax.all_to_all(v, 'ctx', split_axis=0, concat_axis=0, tiled=True)  26.2 us
    pallas_call x2, Pallas kernels, attend_call(): pl.pallas_call(attend_body, grid=(count,), out_shape=(sds((rows, count *...  24.4 us
    all_gather x1, blocking collectives, gather_line(): return lax.all_gather(shard, 'ctx', axis=0, tiled=True)  21.3 us
    all_to_all x6, waiting for transfers between devices, across(): return lax.all_to_all(v, 'ctx', split_axis=0, concat_axis=0, tiled=True)  20.3 us
  transfers between devices with their start and end apart: 83, of which 25 were waited for; matrix products, arithmetic and copies ran while one was open for 11% of the time, Pallas kernels for 39%

profile of v1, /device:TPU:0, one launch (start us, length us, event | category | flops | bytes accessed | tf_op | source)
XLA Modules:
  0.0 420.6 jit_solution(9363884841776619097)
XLA Ops:
  9.6 21.3 %all_gather.6 = bf16[128,3200]{1,0:T(8,128)(2,1)S(1)} all-gather(bf16[32,3200]{1,0:T(8,128)(2,1)S(1)} %concatenate.31), channel_id=1, replica_groups=mesh['dp'=8,'ctx'=4] {'ctx'}, dimensions={0}, use_global_device_ids=true | all-gather | bytes 1024000 | tf_op jit(solution)/shard_map/all_gather | solution.py:853
  48.6 6.2 %collective-permute-done.7.rest_9_ = bf16[128,1536]{1,0:T(8,128)(2,1)S(1)} collective-permute-done((bf16[128,1536]{1,0:T(8,128)(2,1)S(1)}, bf16[128,1536]{1,0:T(8,128)(2,1)S(1)}, u32[]{:S(2)}, u32[]{:S(2)}) %collective-permute-start.7) | collective-permute-done | bytes 393248 | tf_op jit(solution)/shard_map/ppermute | solution.py:784
  54.8 6.2 %collective-permute-done.8.rest_11_ = bf16[128,1536]{1,0:T(8,128)(2,1)S(1)} collective-permute-done((bf16[128,1536]{1,0:T(8,128)(2,1)S(1)}, bf16[128,1536]{1,0:T(8,128)(2,1)S(1)}, u32[]{:S(2)}, u32[]{:S(2)}) %collective-permute-start.8) | collective-permute-done | bytes 393248 | tf_op jit(solution)/shard_map/ppermute | solution.py:784
  85.2 13.7 %collective-permute-done.16.rest_1_ = bf16[128,3200]{1,0:T(8,128)(2,1)S(1)} collective-permute-done((bf16[128,3200]{1,0:T(8,128)(2,1)S(1)}, bf16[128,3200]{1,0:T(8,128)(2,1)S(1)}, u32[]{:S(2)}, u32[]{:S(2)}) %collective-permute-start.16) | collective-permute-done | bytes 819232 | tf_op jit(solution)/shard_map/ppermute | solution.py:784
  113.2 11.3 %qkv.1 = (bf16[512,1024]{1,0:T(8,128)(2,1)}, bf16[512,1024]{1,0:T(8,128)(2,1)}, bf16[512,2048]{1,0:T(8,128)(2,1)}, f32[8,1024]{1,0:T(8,128)}) custom-call(s32[8]{0:T(128)} %fusion.20.perm, f32[512,128]{1,0:T(8,128)} %get-tuple-element.371.cos_ref, f32[512,128]{1,0:T(8,128)} %get-tuple-element.372.sin_ref, bf16[512,1024]{1,0:T(8,128)(2,1)} %bitcast.137, ...), custom_call_target="tpu_custom_call" | custom-call | flops 1 | bytes 1 | tf_op jit(solution)/shard_map/qkv/pallas_call | solution.py:96
  137.0 11.9 %attend.2 = (bf16[512,512]{1,0:T(8,128)(2,1)}, bf16[4,2,1024,512]{3,2,1,0:T(8,128)(2,1)}) custom-call(s32[8]{0:T(128)} %fusion.20.perm, s32[1024,128]{1,0:T(8,128)} %broadcast_in_dim.18.segk_ref, s32[1,512]{1,0:T(1,128)} %bitcast.155, bf16[512,1024]{1,0:T(8,128)(2,1)} %get-tuple-element.450.q_ref, bf16[512,2048]{1,0:T(8,128)(2,1)} %get-tuple-element.451.k0_ref.v0_ref, ...), custom_call_target="tpu_custom_call" | custom-call | flops 1 | bytes 1 | tf_op jit(solution)/shard_map/attend/pallas_call | solution.py:228
  159.7 12.5 %attend.3 = (bf16[512,512]{1,0:T(8,128)(2,1)}, bf16[4,2,1024,512]{3,2,1,0:T(8,128)(2,1)}) custom-call(s32[8]{0:T(128)} %fusion.20.perm, s32[1024,128]{1,0:T(8,128)} %broadcast_in_dim.18.segk_ref, s32[1,512]{1,0:T(1,128)} %bitcast.156, bf16[512,1024]{1,0:T(8,128)(2,1)} %get-tuple-element.450.q_ref, bf16[512,2048]{1,0:T(8,128)(2,1)} %get-tuple-element.451.k0_ref.v0_ref, ...), custom_call_target="tpu_custom_call" | custom-call | flops 1 | bytes 1 | tf_op jit(solution)/shard_map/attend/pallas_call | solution.py:228
  178.1 6.3 %middle.1 = (f32[512,1024]{1,0:T(8,128)}, bf16[512,1024]{1,0:T(8,128)(2,1)}, bf16[512,1024]{1,0:T(8,128)(2,1)}) custom-call(s32[8]{0:T(128)} %fusion.20.perm, f32[8,1024]{1,0:T(8,128)} %get-tuple-element.483.gains_ref, f32[512,128]{1,0:T(8,128)} %broadcast_in_dim.19.keep_ref.refs_0_, bf16[512,1024]{1,0:T(8,128)(2,1)} %bitcast.138, ...), custom_call_target="tpu_custom_call" | custom-call | flops 1 | bytes 1 | tf_op jit(solution)/shard_map/middle/pallas_call | solution.py:96
  185.3 11.8 %gate.1 = (bf16[512,2688]{1,0:T(8,128)(2,1)}, bf16[512,2688]{1,0:T(8,128)(2,1)}, bf16[512,2688]{1,0:T(8,128)(2,1)}) custom-call(s32[8]{0:T(128)} %fusion.20.perm, bf16[512,1024]{1,0:T(8,128)(2,1)} %get-tuple-element.520.b_hbm.refs_0_, bf16[128,3200]{1,0:T(8,128)(2,1)} %copy-done.4, bf16[128,3200]{1,0:T(8,128)(2,1)} %copy-done.7, ...), custom_call_target="tpu_custom_call" | custom-call | flops 1 | bytes 1 | tf_op jit(solution)/shard_map/gate/pallas_call | solution.py:96
  202.0 13.0 %dgate.1 = (bf16[512,2688]{1,0:T(8,128)(2,1)}, bf16[512,2688]{1,0:T(8,128)(2,1)}, bf16[512,1024]{1,0:T(8,128)(2,1)}) custom-call(s32[8]{0:T(128)} %fusion.20.perm, f32[512,128]{1,0:T(8,128)} %broadcast_in_dim.19.keep_ref.refs_0_, bf16[512,1024]{1,0:T(8,128)(2,1)} %bitcast.141, bf16[512,2688]{1,0:T(8,128)(2,1)} %get-tuple-element.494.f1_hbm, ...), custom_call_target="tpu_custom_call" | custom-call | flops 1 | bytes 1 | tf_op jit(solution)/shard_map/dgate/pallas_call | solution.py:96
  216.6 7.7 %grad_x.2 = (bf16[256,2688]{1,0:T(8,128)(2,1)}, bf16[256,2688]{1,0:T(8,128)(2,1)}) custom-call(s32[8]{0:T(128)} %fusion.20.perm, f32[512,128]{1,0:T(8,128)} %broadcast_in_dim.19.keep_ref.refs_0_, f32[512,128]{1,0:T(8,128)} %broadcast_in_dim.20.refs_1_, bf16[512,1024]{1,0:T(8,128)(2,1)} %bitcast.142, bf16[512,1024]{1,0:T(8,128)(2,1)} %collective-permute-done.39.refs_3_, ...), custom_call_target="tpu_custom_call" | custom-call | flops 1 | bytes 1 | tf_op jit(solution)/shard_map/grad_x/pallas_call | solution.py:96
  225.0 4.7 %all-to-all-start.3 = ((bf16[4,128,1024]{2,1,0:T(8,128)(2,1)}), bf16[4,128,1024]{2,1,0:T(8,128)(2,1)S(1)}, u32[]{:S(2)}, u32[]{:S(2)}) async-start(bf16[4,128,1024]{2,1,0:T(8,128)(2,1)} %bitcast.21), calls=%async_computation.3 | async-start | bytes 2097152 | tf_op jit(solution)/shard_map/all_to_all | solution.py:790
  229.7 11.1 %grad_yx.1 = (bf16[256,2688]{1,0:T(8,128)(2,1)}, bf16[256,2688]{1,0:T(8,128)(2,1)}, bf16[256,2688]{1,0:T(8,128)(2,1)}, bf16[256,2688]{1,0:T(8,128)(2,1)}) custom-call(s32[8]{0:T(128)} %fusion.20.perm, bf16[512,1024]{1,0:T(8,128)(2,1)} %get-tuple-element.520.b_hbm.refs_0_, bf16[512,1024]{1,0:T(8,128)(2,1)} %collective-permute-done.40.refs_1_, ...), custom_call_target="tpu_custom_call" | custom-call | flops 1 | bytes 1 | tf_op jit(solution)/shard_map/grad_yx/pallas_call | solution.py:96
  242.3 14.8 %dmiddle.1 = (f32[512,1024]{1,0:T(8,128)}, bf16[512,1024]{1,0:T(8,128)(2,1)}, bf16[512,1024]{1,0:T(8,128)(2,1)}, f32[1,1024]{1,0:T(1,128)}) custom-call(s32[8]{0:T(128)} %fusion.20.perm, f32[8,1024]{1,0:T(8,128)} %get-tuple-element.483.gains_ref, f32[512,128]{1,0:T(8,128)} %broadcast_in_dim.19.keep_ref.refs_0_, bf16[512,1024]{1,0:T(8,128)(2,1)} %bitcast.143, ...), custom_call_target="tpu_custom_call" | custom-call | flops 1 | bytes 1 | tf_op jit(solution)/shard_map/dmiddle/pallas_call | solution.py:96
  262.3 5.0 %grad_y.3 = (bf16[256,1024]{1,0:T(8,128)(2,1)}, bf16[256,1024]{1,0:T(8,128)(2,1)}) custom-call(s32[8]{0:T(128)} %fusion.20.perm, bf16[512,1024]{1,0:T(8,128)(2,1)} %get-tuple-element.508.refs_0_, bf16[512,1024]{1,0:T(8,128)(2,1)} %collective-permute-done.42.refs_1_, bf16[512,1024]{1,0:T(8,128)(2,1)} %get-tuple-element.530.refs_2_, bf16[512,1024]{1,0:T(8,128)(2,1)} %copy-done.42), custom_call_target="tpu_custom_call" | custom-call | flops 1 | bytes 1 | tf_op jit(solution)/shard_map/grad_y/pallas_call | solution.py:96
  268.9 14.2 %dattend.2 = (bf16[512,512]{1,0:T(8,128)(2,1)}, f32[512,512]{1,0:T(8,128)}, f32[512,512]{1,0:T(8,128)}, bf16[512,512]{1,0:T(8,128)(2,1)}, bf16[512,512]{1,0:T(8,128)(2,1)}) custom-call(s32[8]{0:T(128)} %fusion.20.perm, bf16[512,1024]{1,0:T(8,128)(2,1)} %get-tuple-element.450.q_ref, bf16[512,2048]{1,0:T(8,128)(2,1)} %get-tuple-element.451.k0_ref.v0_ref, ...), custom_call_target="tpu_custom_call" | custom-call | flops 1 | bytes 1 | tf_op jit(solution)/shard_map/dattend/pallas_call | solution.py:564
  296.4 5.6 %grad_y.4 = (bf16[256,1536]{1,0:T(8,128)(2,1)}, bf16[256,1536]{1,0:T(8,128)(2,1)}) custom-call(s32[8]{0:T(128)} %fusion.20.perm, bf16[512,1024]{1,0:T(8,128)(2,1)} %get-tuple-element.507.refs_0_, bf16[512,1024]{1,0:T(8,128)(2,1)} %copy-done.6, bf16[512,1536]{1,0:T(8,128)(2,1)} %dqkv.2.refs_2_.da_hbm, bf16[512,1536]{1,0:T(8,128)(2,1)} %copy-done.33), custom_call_target="tpu_custom_call" | custom-call | flops 1 | bytes 1 | tf_op jit(solution)/shard_map/grad_y/pallas_call | solution.py:96
  303.6 14.7 %dattend.3 = (bf16[512,512]{1,0:T(8,128)(2,1)}, f32[512,512]{1,0:T(8,128)}, f32[512,512]{1,0:T(8,128)}, bf16[512,512]{1,0:T(8,128)(2,1)}, bf16[512,512]{1,0:T(8,128)(2,1)}) custom-call(s32[8]{0:T(128)} %fusion.20.perm, bf16[512,1024]{1,0:T(8,128)(2,1)} %get-tuple-element.450.q_ref, bf16[512,2048]{1,0:T(8,128)(2,1)} %get-tuple-element.451.k0_ref.v0_ref, ...), custom_call_target="tpu_custom_call" | custom-call | flops 1 | bytes 1 | tf_op jit(solution)/shard_map/dattend/pallas_call | solution.py:564
  332.7 9.2 %dinput.1 = (bf16[512,1024]{1,0:T(8,128)(2,1)}, f32[1,1024]{1,0:T(1,128)}) custom-call(s32[8]{0:T(128)} %fusion.20.perm, f32[8,1024]{1,0:T(8,128)} %get-tuple-element.483.gains_ref, bf16[512,1024]{1,0:T(8,128)(2,1)} %bitcast.139, f32[512,1024]{1,0:T(8,128)} %get-tuple-element.526.dh1_hbm, bf16[512,1536]{1,0:T(8,128)(2,1)} %dqkv.2.refs_2_.da_hbm, ...), custom_call_target="tpu_custom_call" | custom-call | flops 1 | bytes 1 | tf_op jit(solution)/shard_map/dinput/pallas_call | solution.py:96
  341.9 5.2 %all-to-all-start.4 = ((bf16[4,128,1024]{2,1,0:T(8,128)(2,1)}), bf16[4,128,1024]{2,1,0:T(8,128)(2,1)S(1)}, u32[]{:S(2)}, u32[]{:S(2)}) async-start(bf16[4,128,1024]{2,1,0:T(8,128)(2,1)} %bitcast.151), calls=%async_computation.5 | async-start | bytes 2097152 | tf_op jit(solution)/shard_map/all_to_all | solution.py:790
  349.1 4.5 %grad_x.3 = (bf16[256,768]{1,0:T(8,128)(2,1)}, bf16[256,768]{1,0:T(8,128)(2,1)}) custom-call(s32[8]{0:T(128)} %fusion.20.perm, bf16[512,1024]{1,0:T(8,128)(2,1)} %get-tuple-element.507.refs_0_, bf16[512,1024]{1,0:T(8,128)(2,1)} %copy-done.6, bf16[512,1536]{1,0:T(8,128)(2,1)} %dqkv.3.db_hbm.refs_2_, bf16[512,1536]{1,0:T(8,128)(2,1)} %collective-permute-done.61.refs_3_), custom_call_target="tpu_custom_call" | custom-call | flops 1 | bytes 1 | tf_op jit(solution)/shard_map/grad_x/pallas_call | solution.py:96
  354.3 4.5 %grad_y.5 = (bf16[256,768]{1,0:T(8,128)(2,1)}, bf16[256,768]{1,0:T(8,128)(2,1)}) custom-call(s32[8]{0:T(128)} %fusion.20.perm, bf16[512,1024]{1,0:T(8,128)(2,1)} %get-tuple-element.507.refs_0_, bf16[512,1024]{1,0:T(8,128)(2,1)} %copy-done.6, bf16[512,1536]{1,0:T(8,128)(2,1)} %dqkv.3.db_hbm.refs_2_, bf16[512,1536]{1,0:T(8,128)(2,1)} %collective-permute-done.61.refs_3_), custom_call_target="tpu_custom_call" | custom-call | flops 1 | bytes 1 | tf_op jit(solution)/shard_map/grad_y/pallas_call | solution.py:96
  388.3 4.9 %all-to-all-start.5 = ((bf16[4,32,3072]{2,1,0:T(8,128)(2,1)}), bf16[4,32,3072]{2,1,0:T(8,128)(2,1)S(1)}, u32[]{:S(2)}, u32[]{:S(2)}) async-start(bf16[4,32,3072]{2,1,0:T(8,128)(2,1)} %bitcast.37), calls=%async_computation.7 | async-start | bytes 1572864 | tf_op jit(solution)/shard_map/all_to_all | solution.py:790
  399.3 13.6 %all-to-all-done.5 = bf16[4,32,3072]{2,1,0:T(8,128)(2,1)S(1)} async-done(((bf16[4,32,3072]{2,1,0:T(8,128)(2,1)}), bf16[4,32,3072]{2,1,0:T(8,128)(2,1)S(1)}, u32[]{:S(2)}, u32[]{:S(2)}) %all-to-all-start.5) | async-done | bytes 786464 | tf_op jit(solution)/shard_map/all_to_all | solution.py:790
  (388 shorter events, 171.7 us)
Async XLA Ops:
  7.2 63.4 %all-gather.2.cloned.1.call-start = ((), (), s32[]{:S(2)}) async-start(), calls=%async_computation.9 | async-start | bytes 2048000 | tf_op jit(solution)/shard_map/all_gather | solution.py:853
  8.6 23.9 %collective-permute-start = (bf16[2,128,1024]{2,1,0:T(8,128)(2,1)S(1)}, bf16[2,128,1024]{2,1,0:T(8,128)(2,1)S(1)}, u32[]{:S(2)}, u32[]{:S(2)}) collective-permute-start(bf16[2,128,1024]{2,1,0:T(8,128)(2,1)S(1)} %get-tuple-element.605), channel_id=1, source_target_pairs={{0,4},{4,0},{8,12},{12,8},{16,20},{20,16},{24,28},{28,24},{1,5},{5... | collective-permute-start | bytes 1572872 | tf_op jit(solution)/shard_map/ppermute | solution.py:784
  72.9 29.4 %all-to-all-start = ((bf16[4,128,1024]{2,1,0:T(8,128)(2,1)}), bf16[4,128,1024]{2,1,0:T(8,128)(2,1)S(1)}, u32[]{:S(2)}, u32[]{:S(2)}) async-start(bf16[4,128,1024]{2,1,0:T(8,128)(2,1)} %bitcast.10), calls=%async_computation | async-start | bytes 2097152 | tf_op jit(solution)/shard_map/all_to_all | solution.py:790
  102.4 23.5 %collective-permute-start.18 = (bf16[128,3200]{1,0:T(8,128)(2,1)S(1)}, bf16[128,3200]{1,0:T(8,128)(2,1)}, u32[]{:S(2)}, u32[]{:S(2)}) collective-permute-start(bf16[128,3200]{1,0:T(8,128)(2,1)S(1)} %get-tuple-element.447.rest_0_), channel_id=1, source_target_pairs={{0,16},{4,20},{8,24},{12,28},{16,0},{20,4},{24,8},{28,12},{1,17},{... | collective-permute-start | bytes 2457608 | tf_op jit(solution)/shard_map/ppermute | solution.py:784
  103.9 22.0 %collective-permute-start.20 = (bf16[128,3200]{1,0:T(8,128)(2,1)S(1)}, bf16[128,3200]{1,0:T(8,128)(2,1)}, u32[]{:S(2)}, u32[]{:S(2)}) collective-permute-start(bf16[128,3200]{1,0:T(8,128)(2,1)S(1)} %get-tuple-element.447.rest_0_), channel_id=1, source_target_pairs={{0,4},{4,0},{8,12},{12,8},{16,20},{20,16},{24,28},{28,24},{1,5},{5... | collective-permute-start | bytes 2457608 | tf_op jit(solution)/shard_map/ppermute | solution.py:784
  105.6 23.3 %all-to-all-start.1 = ((bf16[4,32,2688]{2,1,0:T(8,128)(2,1)}), bf16[4,32,2688]{2,1,0:T(8,128)(2,1)}, u32[]{:S(2)}, u32[]{:S(2)}) async-start(bf16[4,32,2688]{2,1,0:T(8,128)(2,1)} %broadcast_in_dim.17), calls=%async_computation.1 | async-start | bytes 1376256 | tf_op jit(solution)/shard_map/all_to_all | solution.py:790
  152.7 23.1 %collective-permute-start.29 = (bf16[128,3200]{1,0:T(8,128)(2,1)}, bf16[128,3200]{1,0:T(8,128)(2,1)S(1)}, u32[]{:S(2)}, u32[]{:S(2)}) collective-permute-start(bf16[128,3200]{1,0:T(8,128)(2,1)} %collective-permute-done.18.rest_2_), channel_id=1, source_target_pairs={{0,4},{4,0},{8,12},{12,8},{16,20},{20,16},{24,28},{28,24},{1,5},{5... | collective-permute-start | bytes 2457608 | tf_op jit(solution)/shard_map/ppermute | solution.py:784
  153.6 22.2 %collective-permute-start.30 = (bf16[128,3200]{1,0:T(8,128)(2,1)}, bf16[128,3200]{1,0:T(8,128)(2,1)}, u32[]{:S(2)}, u32[]{:S(2)}) collective-permute-start(bf16[128,3200]{1,0:T(8,128)(2,1)} %collective-permute-done.19.rest_9_), channel_id=1, source_target_pairs={{0,4},{4,0},{8,12},{12,8},{16,20},{20,16},{24,28},{28,24},{1,5},{5... | collective-permute-start | bytes 2457608 | tf_op jit(solution)/shard_map/ppermute | solution.py:784
  154.1 44.1 %all-to-all-start.2 = ((bf16[4,128,1024]{2,1,0:T(8,128)(2,1)}), bf16[4,128,1024]{2,1,0:T(8,128)(2,1)S(1)}, u32[]{:S(2)}, u32[]{:S(2)}) async-start(bf16[4,128,1024]{2,1,0:T(8,128)(2,1)} %bitcast.148), calls=%async_computation.2 | async-start | bytes 2097152 | tf_op jit(solution)/shard_map/all_to_all | solution.py:790
  224.3 34.3 %collective-permute-start.45 = (bf16[256,2688]{1,0:T(8,128)(2,1)}, bf16[256,2688]{1,0:T(8,128)(2,1)}, u32[]{:S(2)}, u32[]{:S(2)}) collective-permute-start(bf16[256,2688]{1,0:T(8,128)(2,1)} %get-tuple-element.518), channel_id=1, source_target_pairs={{0,8},{4,12},{8,0},{12,4},{16,24},{20,28},{24,16},{28,20},{1,9},{5... | collective-permute-start | bytes 4128776 | tf_op jit(solution)/shard_map/ppermute | solution.py:784
  225.0 43.9 %all-to-all-start.3 = ((bf16[4,128,1024]{2,1,0:T(8,128)(2,1)}), bf16[4,128,1024]{2,1,0:T(8,128)(2,1)S(1)}, u32[]{:S(2)}, u32[]{:S(2)}) async-start(bf16[4,128,1024]{2,1,0:T(8,128)(2,1)} %bitcast.21), calls=%async_computation.3 | async-start | bytes 2097152 | tf_op jit(solution)/shard_map/all_to_all | solution.py:790
  229.7 94.5 %reduce-scatter.4.cloned.1.call-start = ((), (), s32[]{:S(2)}) async-start(), calls=%async_computation.10 | async-start | bytes 860160 | tf_op jit(solution)/shard_map/reduce_scatter | solution.py:1019
  240.8 42.4 %collective-permute-start.49 = (bf16[256,2688]{1,0:T(8,128)(2,1)}, bf16[256,2688]{1,0:T(8,128)(2,1)S(1)}, u32[]{:S(2)}, u32[]{:S(2)}) collective-permute-start(bf16[256,2688]{1,0:T(8,128)(2,1)} %get-tuple-element.524), channel_id=1, source_target_pairs={{0,16},{4,20},{8,24},{12,28},{16,0},{20,4},{24,8},{28,12},{1,17},{... | collective-permute-start | bytes 4128776 | tf_op jit(solution)/shard_map/ppermute | solution.py:784
  257.2 33.5 %collective-permute-start.48 = (bf16[256,2688]{1,0:T(8,128)(2,1)}, bf16[256,2688]{1,0:T(8,128)(2,1)}, u32[]{:S(2)}, u32[]{:S(2)}) collective-permute-start(bf16[256,2688]{1,0:T(8,128)(2,1)} %get-tuple-element.536), channel_id=1, source_target_pairs={{0,8},{4,12},{8,0},{12,4},{16,24},{20,28},{24,16},{28,20},{1,9},{5... | collective-permute-start | bytes 4128776 | tf_op jit(solution)/shard_map/ppermute | solution.py:784
  260.8 31.2 %collective-permute-start.54 = (bf16[128,2688]{1,0:T(8,128)(2,1)}, bf16[128,2688]{1,0:T(8,128)(2,1)}, u32[]{:S(2)}, u32[]{:S(2)}) collective-permute-start(bf16[128,2688]{1,0:T(8,128)(2,1)} %add_convert_fusion.5), channel_id=1, source_target_pairs={{0,16},{4,20},{8,24},{12,28},{16,0},{20,4},{24,8},{28,12},{1,17},{... | collective-permute-start | bytes 2064392 | tf_op jit(solution)/shard_map/ppermute | solution.py:784
  267.3 51.0 %collective-permute-start.56 = (bf16[256,1024]{1,0:T(8,128)(2,1)}, bf16[256,1024]{1,0:T(8,128)(2,1)}, u32[]{:S(2)}, u32[]{:S(2)}) collective-permute-start(bf16[256,1024]{1,0:T(8,128)(2,1)} %get-tuple-element.531), channel_id=1, source_target_pairs={{0,16},{4,20},{8,24},{12,28},{16,0},{20,4},{24,8},{28,12},{1,17},{... | collective-permute-start | bytes 1572872 | tf_op jit(solution)/shard_map/ppermute | solution.py:784
  285.2 36.1 %collective-permute-start.53 = (bf16[128,2688]{1,0:T(8,128)(2,1)}, bf16[128,2688]{1,0:T(8,128)(2,1)}, u32[]{:S(2)}, u32[]{:S(2)}) collective-permute-start(bf16[128,2688]{1,0:T(8,128)(2,1)} %add_convert_fusion.4), channel_id=1, source_target_pairs={{0,8},{4,12},{8,0},{12,4},{16,24},{20,28},{24,16},{28,20},{1,9},{5... | collective-permute-start | bytes 2064392 | tf_op jit(solution)/shard_map/ppermute | solution.py:784
  294.5 54.6 %reduce-scatter.6.cloned.1.call-start = ((), (), s32[]{:S(2)}) async-start(), calls=%async_computation.11 | async-start | bytes 860160 | tf_op jit(solution)/shard_map/reduce_scatter | solution.py:1019
  294.5 34.3 %collective-permute-start.52 = (bf16[128,2688]{1,0:T(8,128)(2,1)S(1)}, bf16[128,2688]{1,0:T(8,128)(2,1)}, u32[]{:S(2)}, u32[]{:S(2)}) collective-permute-start(bf16[128,2688]{1,0:T(8,128)(2,1)S(1)} %add_convert_fusion.3), channel_id=1, source_target_pairs={{0,16},{4,20},{8,24},{12,28},{16,0},{20,4},{24,8},{28,12},{1,17},{... | collective-permute-start | bytes 2064392 | tf_op jit(solution)/shard_map/ppermute | solution.py:784
  302.0 56.8 %collective-permute-start.63 = (bf16[256,1536]{1,0:T(8,128)(2,1)}, bf16[256,1536]{1,0:T(8,128)(2,1)}, u32[]{:S(2)}, u32[]{:S(2)}) collective-permute-start(bf16[256,1536]{1,0:T(8,128)(2,1)} %get-tuple-element.553), channel_id=1, source_target_pairs={{0,16},{4,20},{8,24},{12,28},{16,0},{20,4},{24,8},{28,12},{1,17},{... | collective-permute-start | bytes 2359304 | tf_op jit(solution)/shard_map/ppermute | solution.py:784
  341.9 31.7 %all-to-all-start.4 = ((bf16[4,128,1024]{2,1,0:T(8,128)(2,1)}), bf16[4,128,1024]{2,1,0:T(8,128)(2,1)S(1)}, u32[]{:S(2)}, u32[]{:S(2)}) async-start(bf16[4,128,1024]{2,1,0:T(8,128)(2,1)} %bitcast.151), calls=%async_computation.5 | async-start | bytes 2097152 | tf_op jit(solution)/shard_map/all_to_all | solution.py:790
  347.1 46.6 %reduce-scatter.8.cloned.1.call-start = ((), (), s32[]{:S(2)}) async-start(), calls=%async_computation.12 | async-start | bytes 1187840 | tf_op jit(solution)/shard_map/reduce_scatter | solution.py:1019
  374.5 22.6 %collective-permute-start.60 = (bf16[2,128,1024]{2,1,0:T(8,128)(2,1)}, bf16[2,128,1024]{2,1,0:T(8,128)(2,1)}, u32[]{:S(2)}, u32[]{:S(2)}) collective-permute-start(bf16[2,128,1024]{2,1,0:T(8,128)(2,1)} %select_bitcast_fusion), channel_id=1, source_target_pairs={{0,4},{4,0},{8,12},{12,8},{16,20},{20,16},{24,28},{28,24},{1,5},{5... | collective-permute-start | bytes 1572872 | tf_op jit(solution)/shard_map/ppermute | solution.py:784
  388.3 24.6 %all-to-all-start.5 = ((bf16[4,32,3072]{2,1,0:T(8,128)(2,1)}), bf16[4,32,3072]{2,1,0:T(8,128)(2,1)S(1)}, u32[]{:S(2)}, u32[]{:S(2)}) async-start(bf16[4,32,3072]{2,1,0:T(8,128)(2,1)} %bitcast.37), calls=%async_computation.7 | async-start | bytes 1572864 | tf_op jit(solution)/shard_map/all_to_all | solution.py:790
  (131 other events, 1291.6 us)
Sparse Core Ops, SparseCore 0:
  32.7 37.9 all-gather.1
  294.6 22.8 reduce-scatter.3
  324.2 22.3 reduce-scatter.5
  367.2 24.8 reduce-scatter.7

commit v2 on v1

--- a/solution.py
+++ b/solution.py
@@ -140,7 +140,7 @@
         normed, _ = norm_rows(x[r, :].astype(F32))
         a[r, :] = (normed * gains[0:1, :]).astype(BF16)
 
-    row_tiles(rows, LANE, normalize)
+    row_tiles(rows, 256, normalize)
     done += move.start(a, a_hbm)
     for m in range(width // LANE):
         ap[:, m * LANE : (m + 1) * LANE] = a[:, lanes(perm, m)]
@@ -466,7 +466,7 @@
         at = t * (rows // 2)
 
         def back(i, carry, at=at):
-            r = pl.ds(pl.multiple_of(at + i * LANE, LANE), LANE)
+            r = pl.ds(pl.multiple_of(at + i * 256, 256), 256)
             normed, inv = norm_rows(h1[r, :])
             v = db[r, :]
             gg[...] += jnp.sum(v * normed, axis=0, keepdims=True)
@@ -475,7 +475,7 @@
             e[r, :] = (keep_ref[r, :1] * dh1).astype(BF16)
             return carry
 
-        lax.fori_loop(0, rows // 2 // LANE, back, 0)
+        lax.fori_loop(0, rows // 2 // 256, back, 0)
         part = slice(at, at + rows // 2)
         done += move.start(db.at[part, :], dh1_hbm.at[part, :]) + move.start(e.at[part, :], e_hbm.at[part, :])
         d = nt(e[part, :], wo[...])
@@ -649,14 +649,14 @@
         at = t * (rows // 2)
 
         def back(i, carry, at=at):
-            r = pl.ds(pl.multiple_of(at + i * LANE, LANE), LANE)
+            r = pl.ds(pl.multiple_of(at + i * 256, 256), 256)
             normed, inv = norm_rows(x[r, :].astype(F32))
             v = e[r, :]
             gg[...] += jnp.sum(v * normed, axis=0, keepdims=True)
             out[r, :] = (dh1[r, :] + norm_back(v, gains_ref[0:1, :], normed, inv)).astype(BF16)
             return carry
 
-        lax.fori_loop(0, rows // 2 // LANE, back, 0)
+        lax.fori_loop(0, rows // 2 // 256, back, 0)
         here = slice(at, at + rows // 2)
         done += move.start(out.at[here, :], out_hbm.at[here, :])
     done += move.start(gg, gg_hbm)

time: 426 us -> 425 us (level)
  no operation moved by 1% of the time
where the time goes in v2:
time: 425 us; the launch traced here: 420 us
  Pallas kernels  164 us (39%)
  waiting for transfers between devices  79.8 us (19%)
  starting transfers between devices  73 us (17%)
  other arithmetic  39.9 us (9%)
  local copies, waits for them, and re-layouts  26.7 us (6%)
  blocking collectives  21.3 us (5%)
  between operations  15.2 us (4%)
    pallas_call x12, Pallas kernels, call(): pl.pallas_call(body, out_shape=tuple(outs), in_specs=[SMEM] + [pl.BlockSp...  103 us
    ppermute x71, waiting for transfers between devices, swap(): return lax.ppermute(v, 'dp', [(i, i ^ bit) for i in range(dp_count)])  55.4 us
    ppermute x71, starting transfers between devices, swap(): return lax.ppermute(v, 'dp', [(i, i ^ bit) for i in range(dp_count)])  42.2 us
    pallas_call x2, Pallas kernels, dattend_call(): pl.pallas_call(dattend_body, grid=(count,), out_shape=(sds((rows, count *...  28.4 us
    all_to_all x6, starting transfers between devices, across(): return lax.all_to_all(v, 'ctx', split_axis=0, concat_axis=0, tiled=True)  26.2 us
    pallas_call x2, Pallas kernels, attend_call(): pl.pallas_call(attend_body, grid=(count,), out_shape=(sds((rows, count *...  24.4 us
    all_gather x1, blocking collectives, gather_line(): return lax.all_gather(shard, 'ctx', axis=0, tiled=True)  21.3 us
    all_to_all x6, waiting for transfers between devices, across(): return lax.all_to_all(v, 'ctx', split_axis=0, concat_axis=0, tiled=True)  20.6 us
  transfers between devices with their start and end apart: 83, of which 25 were waited for; matrix products, arithmetic and copies ran while one was open for 11% of the time, Pallas kernels for 39%

profile of v2, /device:TPU:0, one launch (start us, length us, event | category | flops | bytes accessed | tf_op | source)
XLA Modules:
  0.0 419.6 jit_solution(8334166454843047535)
XLA Ops:
  9.6 21.3 %all_gather.6 = bf16[128,3200]{1,0:T(8,128)(2,1)S(1)} all-gather(bf16[32,3200]{1,0:T(8,128)(2,1)S(1)} %concatenate.31), channel_id=1, replica_groups=mesh['dp'=8,'ctx'=4] {'ctx'}, dimensions={0}, use_global_device_ids=true | all-gather | bytes 1024000 | tf_op jit(solution)/shard_map/all_gather | solution.py:853
  48.6 6.2 %collective-permute-done.7.rest_9_ = bf16[128,1536]{1,0:T(8,128)(2,1)S(1)} collective-permute-done((bf16[128,1536]{1,0:T(8,128)(2,1)S(1)}, bf16[128,1536]{1,0:T(8,128)(2,1)S(1)}, u32[]{:S(2)}, u32[]{:S(2)}) %collective-permute-start.7) | collective-permute-done | bytes 393248 | tf_op jit(solution)/shard_map/ppermute | solution.py:784
  54.8 6.2 %collective-permute-done.8.rest_11_ = bf16[128,1536]{1,0:T(8,128)(2,1)S(1)} collective-permute-done((bf16[128,1536]{1,0:T(8,128)(2,1)S(1)}, bf16[128,1536]{1,0:T(8,128)(2,1)S(1)}, u32[]{:S(2)}, u32[]{:S(2)}) %collective-permute-start.8) | collective-permute-done | bytes 393248 | tf_op jit(solution)/shard_map/ppermute | solution.py:784
  85.2 13.7 %collective-permute-done.16.rest_1_ = bf16[128,3200]{1,0:T(8,128)(2,1)S(1)} collective-permute-done((bf16[128,3200]{1,0:T(8,128)(2,1)S(1)}, bf16[128,3200]{1,0:T(8,128)(2,1)S(1)}, u32[]{:S(2)}, u32[]{:S(2)}) %collective-permute-start.16) | collective-permute-done | bytes 819232 | tf_op jit(solution)/shard_map/ppermute | solution.py:784
  113.2 11.0 %qkv.1 = (bf16[512,1024]{1,0:T(8,128)(2,1)}, bf16[512,1024]{1,0:T(8,128)(2,1)}, bf16[512,2048]{1,0:T(8,128)(2,1)}, f32[8,1024]{1,0:T(8,128)}) custom-call(s32[8]{0:T(128)} %fusion.20.perm, f32[512,128]{1,0:T(8,128)} %get-tuple-element.371.cos_ref, f32[512,128]{1,0:T(8,128)} %get-tuple-element.372.sin_ref, bf16[512,1024]{1,0:T(8,128)(2,1)} %bitcast.137, ...), custom_call_target="tpu_custom_call" | custom-call | flops 1 | bytes 1 | tf_op jit(solution)/shard_map/qkv/pallas_call | solution.py:96
  137.0 11.9 %attend.2 = (bf16[512,512]{1,0:T(8,128)(2,1)}, bf16[4,2,1024,512]{3,2,1,0:T(8,128)(2,1)}) custom-call(s32[8]{0:T(128)} %fusion.20.perm, s32[1024,128]{1,0:T(8,128)} %broadcast_in_dim.18.segk_ref, s32[1,512]{1,0:T(1,128)} %bitcast.155, bf16[512,1024]{1,0:T(8,128)(2,1)} %get-tuple-element.450.q_ref, bf16[512,2048]{1,0:T(8,128)(2,1)} %get-tuple-element.451.k0_ref.v0_ref, ...), custom_call_target="tpu_custom_call" | custom-call | flops 1 | bytes 1 | tf_op jit(solution)/shard_map/attend/pallas_call | solution.py:228
  159.7 12.5 %attend.3 = (bf16[512,512]{1,0:T(8,128)(2,1)}, bf16[4,2,1024,512]{3,2,1,0:T(8,128)(2,1)}) custom-call(s32[8]{0:T(128)} %fusion.20.perm, s32[1024,128]{1,0:T(8,128)} %broadcast_in_dim.18.segk_ref, s32[1,512]{1,0:T(1,128)} %bitcast.156, bf16[512,1024]{1,0:T(8,128)(2,1)} %get-tuple-element.450.q_ref, bf16[512,2048]{1,0:T(8,128)(2,1)} %get-tuple-element.451.k0_ref.v0_ref, ...), custom_call_target="tpu_custom_call" | custom-call | flops 1 | bytes 1 | tf_op jit(solution)/shard_map/attend/pallas_call | solution.py:228
  178.1 6.3 %middle.1 = (f32[512,1024]{1,0:T(8,128)}, bf16[512,1024]{1,0:T(8,128)(2,1)}, bf16[512,1024]{1,0:T(8,128)(2,1)}) custom-call(s32[8]{0:T(128)} %fusion.20.perm, f32[8,1024]{1,0:T(8,128)} %get-tuple-element.483.gains_ref, f32[512,128]{1,0:T(8,128)} %broadcast_in_dim.19.keep_ref.refs_0_, bf16[512,1024]{1,0:T(8,128)(2,1)} %bitcast.138, ...), custom_call_target="tpu_custom_call" | custom-call | flops 1 | bytes 1 | tf_op jit(solution)/shard_map/middle/pallas_call | solution.py:96
  185.3 11.8 %gate.1 = (bf16[512,2688]{1,0:T(8,128)(2,1)}, bf16[512,2688]{1,0:T(8,128)(2,1)}, bf16[512,2688]{1,0:T(8,128)(2,1)}) custom-call(s32[8]{0:T(128)} %fusion.20.perm, bf16[512,1024]{1,0:T(8,128)(2,1)} %get-tuple-element.520.b_hbm.refs_0_, bf16[128,3200]{1,0:T(8,128)(2,1)} %copy-done.4, bf16[128,3200]{1,0:T(8,128)(2,1)} %copy-done.7, ...), custom_call_target="tpu_custom_call" | custom-call | flops 1 | bytes 1 | tf_op jit(solution)/shard_map/gate/pallas_call | solution.py:96
  202.0 13.0 %dgate.1 = (bf16[512,2688]{1,0:T(8,128)(2,1)}, bf16[512,2688]{1,0:T(8,128)(2,1)}, bf16[512,1024]{1,0:T(8,128)(2,1)}) custom-call(s32[8]{0:T(128)} %fusion.20.perm, f32[512,128]{1,0:T(8,128)} %broadcast_in_dim.19.keep_ref.refs_0_, bf16[512,1024]{1,0:T(8,128)(2,1)} %bitcast.141, bf16[512,2688]{1,0:T(8,128)(2,1)} %get-tuple-element.494.f1_hbm, ...), custom_call_target="tpu_custom_call" | custom-call | flops 1 | bytes 1 | tf_op jit(solution)/shard_map/dgate/pallas_call | solution.py:96
  216.6 7.7 %grad_x.2 = (bf16[256,2688]{1,0:T(8,128)(2,1)}, bf16[256,2688]{1,0:T(8,128)(2,1)}) custom-call(s32[8]{0:T(128)} %fusion.20.perm, f32[512,128]{1,0:T(8,128)} %broadcast_in_dim.19.keep_ref.refs_0_, f32[512,128]{1,0:T(8,128)} %broadcast_in_dim.20.refs_1_, bf16[512,1024]{1,0:T(8,128)(2,1)} %bitcast.142, bf16[512,1024]{1,0:T(8,128)(2,1)} %collective-permute-done.39.refs_3_, ...), custom_call_target="tpu_custom_call" | custom-call | flops 1 | bytes 1 | tf_op jit(solution)/shard_map/grad_x/pallas_call | solution.py:96
  225.0 4.7 %all-to-all-start.3 = ((bf16[4,128,1024]{2,1,0:T(8,128)(2,1)}), bf16[4,128,1024]{2,1,0:T(8,128)(2,1)S(1)}, u32[]{:S(2)}, u32[]{:S(2)}) async-start(bf16[4,128,1024]{2,1,0:T(8,128)(2,1)} %bitcast.21), calls=%async_computation.3 | async-start | bytes 2097152 | tf_op jit(solution)/shard_map/all_to_all | solution.py:790
  229.7 11.1 %grad_yx.1 = (bf16[256,2688]{1,0:T(8,128)(2,1)}, bf16[256,2688]{1,0:T(8,128)(2,1)}, bf16[256,2688]{1,0:T(8,128)(2,1)}, bf16[256,2688]{1,0:T(8,128)(2,1)}) custom-call(s32[8]{0:T(128)} %fusion.20.perm, bf16[512,1024]{1,0:T(8,128)(2,1)} %get-tuple-element.520.b_hbm.refs_0_, bf16[512,1024]{1,0:T(8,128)(2,1)} %collective-permute-done.40.refs_1_, ...), custom_call_target="tpu_custom_call" | custom-call | flops 1 | bytes 1 | tf_op jit(solution)/shard_map/grad_yx/pallas_call | solution.py:96
  242.3 14.1 %dmiddle.1 = (f32[512,1024]{1,0:T(8,128)}, bf16[512,1024]{1,0:T(8,128)(2,1)}, bf16[512,1024]{1,0:T(8,128)(2,1)}, f32[1,1024]{1,0:T(1,128)}) custom-call(s32[8]{0:T(128)} %fusion.20.perm, f32[8,1024]{1,0:T(8,128)} %get-tuple-element.483.gains_ref, f32[512,128]{1,0:T(8,128)} %broadcast_in_dim.19.keep_ref.refs_0_, bf16[512,1024]{1,0:T(8,128)(2,1)} %bitcast.143, ...), custom_call_target="tpu_custom_call" | custom-call | flops 1 | bytes 1 | tf_op jit(solution)/shard_map/dmiddle/pallas_call | solution.py:96
  262.1 5.0 %grad_y.3 = (bf16[256,1024]{1,0:T(8,128)(2,1)}, bf16[256,1024]{1,0:T(8,128)(2,1)}) custom-call(s32[8]{0:T(128)} %fusion.20.perm, bf16[512,1024]{1,0:T(8,128)(2,1)} %get-tuple-element.508.refs_0_, bf16[512,1024]{1,0:T(8,128)(2,1)} %collective-permute-done.42.refs_1_, bf16[512,1024]{1,0:T(8,128)(2,1)} %get-tuple-element.530.refs_2_, bf16[512,1024]{1,0:T(8,128)(2,1)} %copy-done.42), custom_call_target="tpu_custom_call" | custom-call | flops 1 | bytes 1 | tf_op jit(solution)/shard_map/grad_y/pallas_call | solution.py:96
  268.6 14.2 %dattend.2 = (bf16[512,512]{1,0:T(8,128)(2,1)}, f32[512,512]{1,0:T(8,128)}, f32[512,512]{1,0:T(8,128)}, bf16[512,512]{1,0:T(8,128)(2,1)}, bf16[512,512]{1,0:T(8,128)(2,1)}) custom-call(s32[8]{0:T(128)} %fusion.20.perm, bf16[512,1024]{1,0:T(8,128)(2,1)} %get-tuple-element.450.q_ref, bf16[512,2048]{1,0:T(8,128)(2,1)} %get-tuple-element.451.k0_ref.v0_ref, ...), custom_call_target="tpu_custom_call" | custom-call | flops 1 | bytes 1 | tf_op jit(solution)/shard_map/dattend/pallas_call | solution.py:564
  296.1 5.6 %grad_y.4 = (bf16[256,1536]{1,0:T(8,128)(2,1)}, bf16[256,1536]{1,0:T(8,128)(2,1)}) custom-call(s32[8]{0:T(128)} %fusion.20.perm, bf16[512,1024]{1,0:T(8,128)(2,1)} %get-tuple-element.507.refs_0_, bf16[512,1024]{1,0:T(8,128)(2,1)} %copy-done.6, bf16[512,1536]{1,0:T(8,128)(2,1)} %dqkv.2.refs_2_.da_hbm, bf16[512,1536]{1,0:T(8,128)(2,1)} %copy-done.33), custom_call_target="tpu_custom_call" | custom-call | flops 1 | bytes 1 | tf_op jit(solution)/shard_map/grad_y/pallas_call | solution.py:96
  303.3 14.3 %dattend.3 = (bf16[512,512]{1,0:T(8,128)(2,1)}, f32[512,512]{1,0:T(8,128)}, f32[512,512]{1,0:T(8,128)}, bf16[512,512]{1,0:T(8,128)(2,1)}, bf16[512,512]{1,0:T(8,128)(2,1)}) custom-call(s32[8]{0:T(128)} %fusion.20.perm, bf16[512,1024]{1,0:T(8,128)(2,1)} %get-tuple-element.450.q_ref, bf16[512,2048]{1,0:T(8,128)(2,1)} %get-tuple-element.451.k0_ref.v0_ref, ...), custom_call_target="tpu_custom_call" | custom-call | flops 1 | bytes 1 | tf_op jit(solution)/shard_map/dattend/pallas_call | solution.py:564
  332.0 8.9 %dinput.1 = (bf16[512,1024]{1,0:T(8,128)(2,1)}, f32[1,1024]{1,0:T(1,128)}) custom-call(s32[8]{0:T(128)} %fusion.20.perm, f32[8,1024]{1,0:T(8,128)} %get-tuple-element.483.gains_ref, bf16[512,1024]{1,0:T(8,128)(2,1)} %bitcast.139, f32[512,1024]{1,0:T(8,128)} %get-tuple-element.526.dh1_hbm, bf16[512,1536]{1,0:T(8,128)(2,1)} %dqkv.2.refs_2_.da_hbm, ...), custom_call_target="tpu_custom_call" | custom-call | flops 1 | bytes 1 | tf_op jit(solution)/shard_map/dinput/pallas_call | solution.py:96
  340.9 5.2 %all-to-all-start.4 = ((bf16[4,128,1024]{2,1,0:T(8,128)(2,1)}), bf16[4,128,1024]{2,1,0:T(8,128)(2,1)S(1)}, u32[]{:S(2)}, u32[]{:S(2)}) async-start(bf16[4,128,1024]{2,1,0:T(8,128)(2,1)} %bitcast.151), calls=%async_computation.5 | async-start | bytes 2097152 | tf_op jit(solution)/shard_map/all_to_all | solution.py:790
  348.1 4.5 %grad_x.3 = (bf16[256,768]{1,0:T(8,128)(2,1)}, bf16[256,768]{1,0:T(8,128)(2,1)}) custom-call(s32[8]{0:T(128)} %fusion.20.perm, bf16[512,1024]{1,0:T(8,128)(2,1)} %get-tuple-element.507.refs_0_, bf16[512,1024]{1,0:T(8,128)(2,1)} %copy-done.6, bf16[512,1536]{1,0:T(8,128)(2,1)} %dqkv.3.db_hbm.refs_2_, bf16[512,1536]{1,0:T(8,128)(2,1)} %collective-permute-done.61.refs_3_), custom_call_target="tpu_custom_call" | custom-call | flops 1 | bytes 1 | tf_op jit(solution)/shard_map/grad_x/pallas_call | solution.py:96
  353.3 4.5 %grad_y.5 = (bf16[256,768]{1,0:T(8,128)(2,1)}, bf16[256,768]{1,0:T(8,128)(2,1)}) custom-call(s32[8]{0:T(128)} %fusion.20.perm, bf16[512,1024]{1,0:T(8,128)(2,1)} %get-tuple-element.507.refs_0_, bf16[512,1024]{1,0:T(8,128)(2,1)} %copy-done.6, bf16[512,1536]{1,0:T(8,128)(2,1)} %dqkv.3.db_hbm.refs_2_, bf16[512,1536]{1,0:T(8,128)(2,1)} %collective-permute-done.61.refs_3_), custom_call_target="tpu_custom_call" | custom-call | flops 1 | bytes 1 | tf_op jit(solution)/shard_map/grad_y/pallas_call | solution.py:96
  387.3 4.8 %all-to-all-start.5 = ((bf16[4,32,3072]{2,1,0:T(8,128)(2,1)}), bf16[4,32,3072]{2,1,0:T(8,128)(2,1)S(1)}, u32[]{:S(2)}, u32[]{:S(2)}) async-start(bf16[4,32,3072]{2,1,0:T(8,128)(2,1)} %bitcast.37), calls=%async_computation.7 | async-start | bytes 1572864 | tf_op jit(solution)/shard_map/all_to_all | solution.py:790
  398.3 13.6 %all-to-all-done.5 = bf16[4,32,3072]{2,1,0:T(8,128)(2,1)S(1)} async-done(((bf16[4,32,3072]{2,1,0:T(8,128)(2,1)}), bf16[4,32,3072]{2,1,0:T(8,128)(2,1)S(1)}, u32[]{:S(2)}, u32[]{:S(2)}) %all-to-all-start.5) | async-done | bytes 786464 | tf_op jit(solution)/shard_map/all_to_all | solution.py:790
  (388 shorter events, 172.5 us)
Async XLA Ops:
  7.2 63.4 %all-gather.2.cloned.1.call-start = ((), (), s32[]{:S(2)}) async-start(), calls=%async_computation.9 | async-start | bytes 2048000 | tf_op jit(solution)/shard_map/all_gather | solution.py:853
  8.6 23.9 %collective-permute-start = (bf16[2,128,1024]{2,1,0:T(8,128)(2,1)S(1)}, bf16[2,128,1024]{2,1,0:T(8,128)(2,1)S(1)}, u32[]{:S(2)}, u32[]{:S(2)}) collective-permute-start(bf16[2,128,1024]{2,1,0:T(8,128)(2,1)S(1)} %get-tuple-element.605), channel_id=1, source_target_pairs={{0,4},{4,0},{8,12},{12,8},{16,20},{20,16},{24,28},{28,24},{1,5},{5... | collective-permute-start | bytes 1572872 | tf_op jit(solution)/shard_map/ppermute | solution.py:784
  72.9 29.4 %all-to-all-start = ((bf16[4,128,1024]{2,1,0:T(8,128)(2,1)}), bf16[4,128,1024]{2,1,0:T(8,128)(2,1)S(1)}, u32[]{:S(2)}, u32[]{:S(2)}) async-start(bf16[4,128,1024]{2,1,0:T(8,128)(2,1)} %bitcast.10), calls=%async_computation | async-start | bytes 2097152 | tf_op jit(solution)/shard_map/all_to_all | solution.py:790
  102.4 23.2 %collective-permute-start.18 = (bf16[128,3200]{1,0:T(8,128)(2,1)S(1)}, bf16[128,3200]{1,0:T(8,128)(2,1)}, u32[]{:S(2)}, u32[]{:S(2)}) collective-permute-start(bf16[128,3200]{1,0:T(8,128)(2,1)S(1)} %get-tuple-element.447.rest_0_), channel_id=1, source_target_pairs={{0,16},{4,20},{8,24},{12,28},{16,0},{20,4},{24,8},{28,12},{1,17},{... | collective-permute-start | bytes 2457608 | tf_op jit(solution)/shard_map/ppermute | solution.py:784
  105.6 23.3 %all-to-all-start.1 = ((bf16[4,32,2688]{2,1,0:T(8,128)(2,1)}), bf16[4,32,2688]{2,1,0:T(8,128)(2,1)}, u32[]{:S(2)}, u32[]{:S(2)}) async-start(bf16[4,32,2688]{2,1,0:T(8,128)(2,1)} %broadcast_in_dim.17), calls=%async_computation.1 | async-start | bytes 1376256 | tf_op jit(solution)/shard_map/all_to_all | solution.py:790
  152.7 23.1 %collective-permute-start.29 = (bf16[128,3200]{1,0:T(8,128)(2,1)}, bf16[128,3200]{1,0:T(8,128)(2,1)S(1)}, u32[]{:S(2)}, u32[]{:S(2)}) collective-permute-start(bf16[128,3200]{1,0:T(8,128)(2,1)} %collective-permute-done.18.rest_2_), channel_id=1, source_target_pairs={{0,4},{4,0},{8,12},{12,8},{16,20},{20,16},{24,28},{28,24},{1,5},{5... | collective-permute-start | bytes 2457608 | tf_op jit(solution)/shard_map/ppermute | solution.py:784
  153.6 22.2 %collective-permute-start.30 = (bf16[128,3200]{1,0:T(8,128)(2,1)}, bf16[128,3200]{1,0:T(8,128)(2,1)}, u32[]{:S(2)}, u32[]{:S(2)}) collective-permute-start(bf16[128,3200]{1,0:T(8,128)(2,1)} %collective-permute-done.19.rest_9_), channel_id=1, source_target_pairs={{0,4},{4,0},{8,12},{12,8},{16,20},{20,16},{24,28},{28,24},{1,5},{5... | collective-permute-start | bytes 2457608 | tf_op jit(solution)/shard_map/ppermute | solution.py:784
  153.8 22.0 %collective-permute-start.31 = (bf16[128,3200]{1,0:T(8,128)(2,1)}, bf16[128,3200]{1,0:T(8,128)(2,1)S(1)}, u32[]{:S(2)}, u32[]{:S(2)}) collective-permute-start(bf16[128,3200]{1,0:T(8,128)(2,1)} %collective-permute-done.23.rest_3_), channel_id=1, source_target_pairs={{0,4},{4,0},{8,12},{12,8},{16,20},{20,16},{24,28},{28,24},{1,5},{5... | collective-permute-start | bytes 2457608 | tf_op jit(solution)/shard_map/ppermute | solution.py:784
  154.1 44.1 %all-to-all-start.2 = ((bf16[4,128,1024]{2,1,0:T(8,128)(2,1)}), bf16[4,128,1024]{2,1,0:T(8,128)(2,1)S(1)}, u32[]{:S(2)}, u32[]{:S(2)}) async-start(bf16[4,128,1024]{2,1,0:T(8,128)(2,1)} %bitcast.148), calls=%async_computation.2 | async-start | bytes 2097152 | tf_op jit(solution)/shard_map/all_to_all | solution.py:790
  224.3 33.7 %collective-permute-start.45 = (bf16[256,2688]{1,0:T(8,128)(2,1)}, bf16[256,2688]{1,0:T(8,128)(2,1)}, u32[]{:S(2)}, u32[]{:S(2)}) collective-permute-start(bf16[256,2688]{1,0:T(8,128)(2,1)} %get-tuple-element.518), channel_id=1, source_target_pairs={{0,8},{4,12},{8,0},{12,4},{16,24},{20,28},{24,16},{28,20},{1,9},{5... | collective-permute-start | bytes 4128776 | tf_op jit(solution)/shard_map/ppermute | solution.py:784
  225.0 43.6 %all-to-all-start.3 = ((bf16[4,128,1024]{2,1,0:T(8,128)(2,1)}), bf16[4,128,1024]{2,1,0:T(8,128)(2,1)S(1)}, u32[]{:S(2)}, u32[]{:S(2)}) async-start(bf16[4,128,1024]{2,1,0:T(8,128)(2,1)} %bitcast.21), calls=%async_computation.3 | async-start | bytes 2097152 | tf_op jit(solution)/shard_map/all_to_all | solution.py:790
  229.7 93.7 %reduce-scatter.4.cloned.1.call-start = ((), (), s32[]{:S(2)}) async-start(), calls=%async_computation.10 | async-start | bytes 860160 | tf_op jit(solution)/shard_map/reduce_scatter | solution.py:1019
  240.8 42.1 %collective-permute-start.49 = (bf16[256,2688]{1,0:T(8,128)(2,1)}, bf16[256,2688]{1,0:T(8,128)(2,1)S(1)}, u32[]{:S(2)}, u32[]{:S(2)}) collective-permute-start(bf16[256,2688]{1,0:T(8,128)(2,1)} %get-tuple-element.524), channel_id=1, source_target_pairs={{0,16},{4,20},{8,24},{12,28},{16,0},{20,4},{24,8},{28,12},{1,17},{... | collective-permute-start | bytes 4128776 | tf_op jit(solution)/shard_map/ppermute | solution.py:784
  256.5 33.9 %collective-permute-start.48 = (bf16[256,2688]{1,0:T(8,128)(2,1)}, bf16[256,2688]{1,0:T(8,128)(2,1)}, u32[]{:S(2)}, u32[]{:S(2)}) collective-permute-start(bf16[256,2688]{1,0:T(8,128)(2,1)} %get-tuple-element.536), channel_id=1, source_target_pairs={{0,8},{4,12},{8,0},{12,4},{16,24},{20,28},{24,16},{28,20},{1,9},{5... | collective-permute-start | bytes 4128776 | tf_op jit(solution)/shard_map/ppermute | solution.py:784
  260.5 31.2 %collective-permute-start.54 = (bf16[128,2688]{1,0:T(8,128)(2,1)}, bf16[128,2688]{1,0:T(8,128)(2,1)}, u32[]{:S(2)}, u32[]{:S(2)}) collective-permute-start(bf16[128,2688]{1,0:T(8,128)(2,1)} %add_convert_fusion.5), channel_id=1, source_target_pairs={{0,16},{4,20},{8,24},{12,28},{16,0},{20,4},{24,8},{28,12},{1,17},{... | collective-permute-start | bytes 2064392 | tf_op jit(solution)/shard_map/ppermute | solution.py:784
  267.1 50.5 %collective-permute-start.56 = (bf16[256,1024]{1,0:T(8,128)(2,1)}, bf16[256,1024]{1,0:T(8,128)(2,1)}, u32[]{:S(2)}, u32[]{:S(2)}) collective-permute-start(bf16[256,1024]{1,0:T(8,128)(2,1)} %get-tuple-element.531), channel_id=1, source_target_pairs={{0,16},{4,20},{8,24},{12,28},{16,0},{20,4},{24,8},{28,12},{1,17},{... | collective-permute-start | bytes 1572872 | tf_op jit(solution)/shard_map/ppermute | solution.py:784
  285.0 35.6 %collective-permute-start.53 = (bf16[128,2688]{1,0:T(8,128)(2,1)}, bf16[128,2688]{1,0:T(8,128)(2,1)}, u32[]{:S(2)}, u32[]{:S(2)}) collective-permute-start(bf16[128,2688]{1,0:T(8,128)(2,1)} %add_convert_fusion.4), channel_id=1, source_target_pairs={{0,8},{4,12},{8,0},{12,4},{16,24},{20,28},{24,16},{28,20},{1,9},{5... | collective-permute-start | bytes 2064392 | tf_op jit(solution)/shard_map/ppermute | solution.py:784
  294.2 53.9 %reduce-scatter.6.cloned.1.call-start = ((), (), s32[]{:S(2)}) async-start(), calls=%async_computation.11 | async-start | bytes 860160 | tf_op jit(solution)/shard_map/reduce_scatter | solution.py:1019
  294.3 33.9 %collective-permute-start.52 = (bf16[128,2688]{1,0:T(8,128)(2,1)S(1)}, bf16[128,2688]{1,0:T(8,128)(2,1)}, u32[]{:S(2)}, u32[]{:S(2)}) collective-permute-start(bf16[128,2688]{1,0:T(8,128)(2,1)S(1)} %add_convert_fusion.3), channel_id=1, source_target_pairs={{0,16},{4,20},{8,24},{12,28},{16,0},{20,4},{24,8},{28,12},{1,17},{... | collective-permute-start | bytes 2064392 | tf_op jit(solution)/shard_map/ppermute | solution.py:784
  301.8 56.1 %collective-permute-start.63 = (bf16[256,1536]{1,0:T(8,128)(2,1)}, bf16[256,1536]{1,0:T(8,128)(2,1)}, u32[]{:S(2)}, u32[]{:S(2)}) collective-permute-start(bf16[256,1536]{1,0:T(8,128)(2,1)} %get-tuple-element.553), channel_id=1, source_target_pairs={{0,16},{4,20},{8,24},{12,28},{16,0},{20,4},{24,8},{28,12},{1,17},{... | collective-permute-start | bytes 2359304 | tf_op jit(solution)/shard_map/ppermute | solution.py:784
  340.9 31.7 %all-to-all-start.4 = ((bf16[4,128,1024]{2,1,0:T(8,128)(2,1)}), bf16[4,128,1024]{2,1,0:T(8,128)(2,1)S(1)}, u32[]{:S(2)}, u32[]{:S(2)}) async-start(bf16[4,128,1024]{2,1,0:T(8,128)(2,1)} %bitcast.151), calls=%async_computation.5 | async-start | bytes 2097152 | tf_op jit(solution)/shard_map/all_to_all | solution.py:790
  346.1 46.6 %reduce-scatter.8.cloned.1.call-start = ((), (), s32[]{:S(2)}) async-start(), calls=%async_computation.12 | async-start | bytes 1187840 | tf_op jit(solution)/shard_map/reduce_scatter | solution.py:1019
  373.5 22.6 %collective-permute-start.60 = (bf16[2,128,1024]{2,1,0:T(8,128)(2,1)}, bf16[2,128,1024]{2,1,0:T(8,128)(2,1)}, u32[]{:S(2)}, u32[]{:S(2)}) collective-permute-start(bf16[2,128,1024]{2,1,0:T(8,128)(2,1)} %select_bitcast_fusion), channel_id=1, source_target_pairs={{0,4},{4,0},{8,12},{12,8},{16,20},{20,16},{24,28},{28,24},{1,5},{5... | collective-permute-start | bytes 1572872 | tf_op jit(solution)/shard_map/ppermute | solution.py:784
  387.3 24.6 %all-to-all-start.5 = ((bf16[4,32,3072]{2,1,0:T(8,128)(2,1)}), bf16[4,32,3072]{2,1,0:T(8,128)(2,1)S(1)}, u32[]{:S(2)}, u32[]{:S(2)}) async-start(bf16[4,32,3072]{2,1,0:T(8,128)(2,1)} %bitcast.37), calls=%async_computation.7 | async-start | bytes 1572864 | tf_op jit(solution)/shard_map/all_to_all | solution.py:790
  (131 other events, 1288.9 us)
Sparse Core Ops, SparseCore 0:
  32.7 37.9 all-gather.1
  294.4 22.6 reduce-scatter.3
  323.5 22.3 reduce-scatter.5
  366.2 24.8 reduce-scatter.7
